TPU v7x, 512 devices: a whole 4x8x8 slice. The times are simulated.
512 devices in a mesh: grp: 16 (over z, y_lo), col: 32 (over x, y_hi, core).
Axes of the slice: x: 4, y: 8 (y_hi: 4, y_lo: 2; y = y_hi * 2 + y_lo), z: 8, core: 2. Of those that a mesh axis runs over, the one named last changes fastest.
Arguments:
- descriptors: bfloat16 [10, 32, 128, 4096], P(None, None, 'grp', 'col'), may hold values from -6 to 6
- solid_temp: float32 [32, 128, 4096], P(None, 'grp', 'col'), may hold values from -6 to 6
- fluid_temp: float32 [32, 128, 4096], P(None, 'grp', 'col'), may hold values from -6 to 6
- material: int32 [32, 128, 4096], P(None, 'grp', 'col'), may hold values from 0 to 3
- fixed_mask: int32 [32, 128, 4096], P(None, 'grp', 'col'), may hold values 0 or 1
- solid_cond: float32 [4], replicated, may hold values from 0.3 to 1.5
- fluid_cond: float32 [4], replicated, may hold values from 0.3 to 1.5
- w_in: bfloat16 [12, 64], replicated, may hold values from -1.75 to 1.75
- b_in: float32 [64], replicated, may hold values from -3 to 3
- w_mid: bfloat16 [64, 64], replicated, may hold values from -0.75 to 0.75
- b_mid: float32 [64], replicated, may hold values from -3 to 3
- w_out: bfloat16 [64, 2], replicated, may hold values from -0.75 to 0.75
- b_out: float32 [2], replicated, may hold values from -3 to 3
- solid_cot: float32 [32, 128, 4096], P(None, 'grp', 'col'), may hold values from -18 to 18
- fluid_cot: float32 [32, 128, 4096], P(None, 'grp', 'col'), may hold values from -18 to 18
Outputs:
- adj_solid: float32 [32, 128, 4096], P(None, 'grp', 'col')
- adj_fluid: float32 [32, 128, 4096], P(None, 'grp', 'col')
- grad_w_in: float32 [12, 64], replicated
- grad_b_in: float32 [64], replicated
- grad_w_mid: float32 [64, 64], replicated
- grad_b_mid: float32 [64], replicated
- grad_w_out: float32 [64, 2], replicated
- grad_b_out: float32 [2], replicated
All inputs are finite; a program needn't handle non-finite values. No bound on the sum of `fixed_mask` on one device may be relied on, other than what follows from the above.
Results may differ from a plain program's by a relative error of at most 0.01.
The roundings to bfloat16 on the way count: a program that leaves them out, or rounds other values in their place, can miss the bound.
Values sent between devices are 32-bit elements; how exact they have to be, the bound alone decides.
No kernel may reach another device: no remote copies, remote signals or barrier semaphores. Data moves between devices by JAX's collectives and lax.ppermute only.
A program may use at most 64 MiB of HBM per device.

v0:
```python
import math

import jax
import jax.numpy as jnp
from jax import lax
from jax.sharding import PartitionSpec as P

time_step = 0.15
loss_gain = 16.0


def padded_2(block, sides, width):
    for axis, dim in sides:
        count = lax.axis_size(axis)
        forward = [(i, i + 1) for i in range(count - 1)]
        backward = [(target, source) for source, target in forward]
        low = lax.ppermute(
            lax.slice_in_dim(block, block.shape[dim] - width, None, axis=dim), axis, forward
        )
        high = lax.ppermute(lax.slice_in_dim(block, 0, width, axis=dim), axis, backward)
        block = jnp.concatenate([low, block, high], axis=dim)
    return block


def material_lookup(material, lookup_table):
    summed = jnp.zeros(material.shape, jnp.float32)
    for material_kind in range(lookup_table.shape[0]):
        summed = summed + jnp.where(material == material_kind, lookup_table[material_kind], 0.0)
    return summed


def neighbour_sum(padded, values_field):
    return (
        padded[:, :, 2:, 1:-1]
        + padded[:, :, :-2, 1:-1]
        + padded[:, :, 1:-1, 2:]
        + padded[:, :, 1:-1, :-2]
        - 4.0 * values_field
    )


def network(features, w_in, b_in, w_mid, b_mid, w_out, b_out):
    hidden_one = jnp.tanh(
        jnp.dot(w_in.T, features, preferred_element_type=jnp.float32) + b_in[:, None]
    ).astype(jnp.bfloat16)
    hidden_two = jnp.tanh(
        jnp.dot(w_mid.T, hidden_one, preferred_element_type=jnp.float32) + b_mid[:, None]
    ).astype(jnp.bfloat16)
    logits = jnp.dot(w_out.T, hidden_two, preferred_element_type=jnp.float32) + b_out[:, None]
    return (hidden_one, hidden_two, logits)


def coupling_terms(logits):
    transfer_coef = jax.nn.softplus(logits[0])
    area_coef = jax.nn.softplus(logits[1])
    return (transfer_coef * area_coef, transfer_coef, area_coef)


def backprop(features, hidden_one, hidden_two, logits, d_coupling, w_in, w_mid, w_out):
    coupling, transfer_coef, area_coef = coupling_terms(logits)
    d_logits = jnp.stack(
        [
            d_coupling * area_coef * jax.nn.sigmoid(logits[0]),
            d_coupling * transfer_coef * jax.nn.sigmoid(logits[1]),
        ]
    ).astype(jnp.bfloat16)
    d_hidden_two = (
        jnp.dot(w_out, d_logits, preferred_element_type=jnp.float32)
        * (1.0 - jnp.square(hidden_two.astype(jnp.float32)))
    ).astype(jnp.bfloat16)
    d_hidden_one = (
        jnp.dot(w_mid, d_hidden_two, preferred_element_type=jnp.float32)
        * (1.0 - jnp.square(hidden_one.astype(jnp.float32)))
    ).astype(jnp.bfloat16)
    d_features = jnp.dot(
        w_in[w_in.shape[0] - 2 :], d_hidden_one, preferred_element_type=jnp.float32
    )
    gradients = (
        jnp.dot(features, d_hidden_one.T, preferred_element_type=jnp.float32),
        jnp.sum(d_hidden_one.astype(jnp.float32), axis=1),
        jnp.dot(hidden_one, d_hidden_two.T, preferred_element_type=jnp.float32),
        jnp.sum(d_hidden_two.astype(jnp.float32), axis=1),
        jnp.dot(hidden_two, d_logits.T, preferred_element_type=jnp.float32),
        jnp.sum(d_logits.astype(jnp.float32), axis=1),
    )
    return (coupling, d_features, gradients)


def build_features(desc_line, solid_line, fluid_line):
    cells = solid_line.size
    return jnp.concatenate(
        [
            desc_line.reshape(desc_line.shape[0], cells),
            solid_line.reshape(1, cells).astype(jnp.bfloat16),
            fluid_line.reshape(1, cells).astype(jnp.bfloat16),
        ],
        axis=0,
    )


def forward_coupling(descriptors, solid, fluid, weights):

    def forward_one_line(line_index):
        desc_line = lax.dynamic_index_in_dim(descriptors, line_index, 1, keepdims=False)
        solid_line = lax.dynamic_index_in_dim(solid, line_index, 0, keepdims=False)
        fluid_line = lax.dynamic_index_in_dim(fluid, line_index, 0, keepdims=False)
        features = build_features(desc_line, solid_line, fluid_line)
        logits = network(features, *weights)[2]
        return coupling_terms(logits)[0].reshape(solid_line.shape)

    return lax.map(forward_one_line, jnp.arange(solid.shape[0], dtype=jnp.int32))


def backward_lines(descriptors, solid, fluid, d_coupling, weights, running):
    w_in, b_in, w_mid, b_mid, w_out, b_out = weights

    def backward_one_line(running, line_index):
        desc_line = lax.dynamic_index_in_dim(descriptors, line_index, 1, keepdims=False)
        solid_line = lax.dynamic_index_in_dim(solid, line_index, 0, keepdims=False)
        fluid_line = lax.dynamic_index_in_dim(fluid, line_index, 0, keepdims=False)
        d_line = lax.dynamic_index_in_dim(d_coupling, line_index, 0, keepdims=False)
        features = build_features(desc_line, solid_line, fluid_line)
        hidden_one, hidden_two, logits = network(features, *weights)
        coupling, d_features, gradients = backprop(
            features, hidden_one, hidden_two, logits, d_line.reshape(-1), w_in, w_mid, w_out
        )
        running = tuple((left + right for left, right in zip(running, gradients)))
        line_shape = solid_line.shape
        return (running, (coupling.reshape(line_shape), d_features.reshape((2,) + line_shape)))

    running, (coupling, d_features) = lax.scan(
        backward_one_line, running, jnp.arange(solid.shape[0], dtype=jnp.int32)
    )
    return (running, coupling, jnp.moveaxis(d_features, 1, 0))


def advance(state, state_padded, conduct, free_cell, first_coupling):
    coupled = first_coupling * (state[1] - state[0])
    return state + time_step * free_cell * (
        conduct * neighbour_sum(state_padded, state) + jnp.stack([coupled, -coupled])
    )


def shards(
    descriptors,
    solid_temp,
    fluid_temp,
    material,
    fixed_mask,
    solid_cond,
    fluid_cond,
    w_in,
    b_in,
    w_mid,
    b_mid,
    w_out,
    b_out,
    solid_cot,
    fluid_cot,
):
    weights = (w_in, b_in, w_mid, b_mid, w_out, b_out)
    conduct = jnp.stack(
        [material_lookup(material, solid_cond), material_lookup(material, fluid_cond)]
    )
    free_cell = 1.0 - fixed_mask.astype(jnp.float32)
    state = jnp.stack([solid_temp, fluid_temp])
    first_coupling = forward_coupling(descriptors, state[0], state[1], weights)
    cotangent = jnp.stack([solid_cot, fluid_cot])
    upstream = time_step * free_cell * cotangent
    pushed = conduct * upstream
    state_padded = padded_2(state, (("grp", 2), ("col", 3)), 1)
    later = advance(state, state_padded, conduct, free_cell, first_coupling)
    pushed_rim = padded_2(pushed, (("grp", 2), ("col", 3)), 1)
    running = (
        jnp.zeros(w_in.shape, jnp.float32),
        jnp.zeros(b_in.shape, jnp.float32),
        jnp.zeros(w_mid.shape, jnp.float32),
        jnp.zeros(b_mid.shape, jnp.float32),
        jnp.zeros(w_out.shape, jnp.float32),
        jnp.zeros(b_out.shape, jnp.float32),
    )
    d_coupling = (later[1] - later[0]) * (upstream[0] - upstream[1])
    running, coupling, d_features = backward_lines(
        descriptors, later[0], later[1], d_coupling, weights, running
    )
    swing_term = coupling * (upstream[1] - upstream[0])
    cotangent = (
        cotangent
        + neighbour_sum(pushed_rim, pushed)
        + jnp.stack([swing_term, -swing_term])
        + d_features
    )
    upstream = time_step * free_cell * cotangent
    pushed = conduct * upstream
    pushed_rim = padded_2(pushed, (("grp", 2), ("col", 3)), 1)
    d_coupling = (state[1] - state[0]) * (upstream[0] - upstream[1])
    running, coupling, d_features = backward_lines(
        descriptors, state[0], state[1], d_coupling, weights, running
    )
    swing_term = coupling * (upstream[1] - upstream[0])
    cotangent = (
        cotangent
        + neighbour_sum(pushed_rim, pushed)
        + jnp.stack([swing_term, -swing_term])
        + d_features
    )
    summed = lax.psum(
        (running[0], running[1], running[2], running[3], running[4], running[5]), ("grp", "col")
    )
    cell_count = solid_temp.size * lax.axis_size("grp") * lax.axis_size("col")
    scale = loss_gain / math.sqrt(cell_count)
    return (
        cotangent[0],
        cotangent[1],
        summed[0] * scale,
        summed[1] * scale,
        summed[2] * scale,
        summed[3] * scale,
        summed[4] * scale,
        summed[5] * scale,
    )


def solution(mesh):
    placed = (
        P(None, None, "grp", "col"),
        P(None, "grp", "col"),
        P(None, "grp", "col"),
        P(None, "grp", "col"),
        P(None, "grp", "col"),
        P(),
        P(),
        P(),
        P(),
        P(),
        P(),
        P(),
        P(),
        P(None, "grp", "col"),
        P(None, "grp", "col"),
    )
    return jax.shard_map(
        shards,
        mesh=mesh,
        in_specs=placed,
        out_specs=(P(None, "grp", "col"), P(None, "grp", "col"), P(), P(), P(), P(), P(), P()),
        check_vma=False,
    )
```

profile of v0, /device:TPU:57, one launch (start us, length us, event | category | flops | bytes accessed | tf_op | source)
XLA Modules:
  0.0 923.3 jit_solution(6519059867842374332)
XLA Ops:
  0.7 1.2 fusion.89
  1.9 3.0 collective-permute-start.4
  4.8 3.7 collective-permute-start.5
  9.8 2.7 add_bitcast_fusion.1
  12.6 2.7 add_bitcast_fusion
  15.4 1.9 collective-permute-start
  17.3 4.3 collective-permute-start.1
  22.4 128.7 %while.59 = (s32[]{:T(128)}, f32[32,8,128]{2,1,0:T(8,128)S(1)}, s32[32]{0:T(128)S(1)}, bf16[10,32,8,128]{3,2,1,0:T(8,128)(2,1)}, bf16[32,8,128]{2,1,0:T(8,128)(2...) while((s32[]{:T(128)}, f32[32,8,128]{2,1,0:T(8,128)S(1)}, ...), condition=%wide.region_1.2_spmd, body=%wide.region_0.1_spmd.sunk | while | flops 10574853 | bytes 510433 | solution.py:111
  152.2 4.5 collective-permute-start.7
  156.7 1.9 collective-permute-start.6
  159.3 1.2 fusion.96
  160.4 6.6 collective-permute-start.3
  167.1 1.9 collective-permute-start.2
  169.0 6.5 collective-permute-done.6
  176.7 415.8 %while.61 = (s32[]{:T(128)}, f32[12,64]{1,0:T(8,128)S(1)}, f32[64]{0:T(128)}, f32[64,64]{1,0:T(8,128)S(1)}, f32[64]{0:T(128)}, /*index=5*/f32[64,2]{0,1:T(2,128)...) while((s32[]{:T(128)}, f32[12,64]{1,0:T(8,128)S(1)}, ...), condition=%wide.region_6.7_spmd.clone, body=%wide.region_2.6_spmd.clone.sunk | while | flops 30749576 | bytes 3280900 | solution.py:131
  572.9 0.9 convert_reduce_fusion.16
  594.3 1.9 collective-permute-start.8
  596.3 4.3 collective-permute-start.9
  601.3 195.9 %while.60 = (s32[]{:T(128)}, f32[12,64]{1,0:T(8,128)S(1)}, f32[64]{0:T(128)S(1)}, f32[64,64]{1,0:T(8,128)S(1)}, f32[64]{0:T(128)S(1)}, /*index=5*/f32[64,2]{0,1:...) while((s32[]{:T(128)}, f32[12,64]{1,0:T(8,128)S(1)}, ...), condition=%wide.region_11.12_spmd, body=%wide.region_7.11_spmd.sunk | while | flops 30744452 | bytes 2216265 | solution.py:131
  797.3 101.6 %all-reduce = (f32[12,64]{1,0:T(8,128)S(1)}, f32[64]{0:T(128)S(1)}, f32[64,64]{1,0:T(8,128)S(1)}, f32[64]{0:T(128)S(1)}, f32[64,2]{0,1:T(2,128)S(1)}, /*index=5*/f32[2]{0:T(128)S(1)}) all-reduce(f32[12,64]{1,0:T(8,128)S(1)} %get-tuple-element.299, f32[64]{0:T(128)S(1)} %get-tuple-element.300, ...), channel_id=1, replica_groups=mesh['grp'=16,'col'=32] {'grp','col'}, use_global_device_ids=true, to_apply=%region_12.13 | all-reduce | flops 5122 | bytes 40976 | tf_op jit(solution)/shard_map/psum | solution.py:207
  902.1 5.3 collective-permute-start.11
  907.4 1.9 collective-permute-start.10
  909.8 8.8 collective-permute-done.11
  918.6 3.5 collective-permute-done.10
  (3336 shorter events, 562.7 us)
Async XLA Ops:
  0.6 9.2 copy-start.7
  0.6 9.2 copy-start.8
  1.8 6.7 copy-start.31
  1.9 150.0 %collective-permute-start.4 = (f32[2,32,1,128]{3,2,1,0:T(1,128)S(1)}, f32[2,32,1,128]{3,2,1,0:T(1,128)S(1)}, u32[]{:S(2)}, u32[]{:S(2)}) collective-permute-start(f32[2,32,1,128]{3,2,1,0:T(1,128)S(1)} %get-tuple-element.537), channel_id=1, source_target_pairs={{32,0},{64,32},{96,64},{128,96},{160,128},{192,160},{224,192},{256... | collective-permute-start | bytes 98312 | tf_op jit(solution)/shard_map/ppermute | solution.py:20
  4.8 147.0 %collective-permute-start.5 = (f32[2,32,1,128]{3,2,1,0:T(1,128)S(1)}, f32[2,32,1,128]{3,2,1,0:T(1,128)S(1)}, u32[]{:S(2)}, u32[]{:S(2)}) collective-permute-start(f32[2,32,1,128]{3,2,1,0:T(1,128)S(1)} %get-tuple-element.536), channel_id=1, source_target_pairs={{0,32},{32,64},{64,96},{96,128},{128,160},{160,192},{192,224},{224... | collective-permute-start | bytes 98312 | tf_op jit(solution)/shard_map/ppermute | solution.py:17
  15.3 6.3 copy-start.1
  15.4 143.2 %collective-permute-start = (f32[2,32,1,128]{3,2,1,0:T(1,128)S(1)}, f32[2,32,1,128]{3,2,1,0:T(1,128)S(1)}, u32[]{:S(2)}, u32[]{:S(2)}) collective-permute-start(f32[2,32,1,128]{3,2,1,0:T(1,128)S(1)} %get-tuple-element.533), channel_id=1, source_target_pairs={{32,0},{64,32},{96,64},{128,96},{160,128},{192,160},{224,192},{256... | collective-permute-start | bytes 98312 | tf_op jit(solution)/shard_map/ppermute | solution.py:20
  17.3 141.3 %collective-permute-start.1 = (f32[2,32,1,128]{3,2,1,0:T(1,128)S(1)}, f32[2,32,1,128]{3,2,1,0:T(1,128)S(1)}, u32[]{:S(2)}, u32[]{:S(2)}) collective-permute-start(f32[2,32,1,128]{3,2,1,0:T(1,128)S(1)} %get-tuple-element.532), channel_id=1, source_target_pairs={{0,32},{32,64},{64,96},{96,128},{128,160},{160,192},{192,224},{224... | collective-permute-start | bytes 98312 | tf_op jit(solution)/shard_map/ppermute | solution.py:17
  152.2 16.8 %collective-permute-start.7 = (f32[2,32,10,1]{3,2,1,0:T(8,128)S(1)}, f32[2,32,10,1]{3,2,1,0:T(8,128)S(1)}, u32[]{:S(2)}, u32[]{:S(2)}) collective-permute-start(f32[2,32,10,1]{3,2,1,0:T(8,128)S(1)} %get-tuple-element.523), channel_id=1, source_target_pairs={{0,1},{1,2},{2,3},{3,4},{4,5},{5,6},{6,7},{7,8},{8,9},{9,10},{10,1... | collective-permute-start | bytes 7688 | tf_op jit(solution)/shard_map/ppermute | solution.py:17
  156.7 18.8 %collective-permute-start.6 = (f32[2,32,10,1]{3,2,1,0:T(8,128)S(1)}, f32[2,32,10,1]{3,2,1,0:T(8,128)S(1)}, u32[]{:S(2)}, u32[]{:S(2)}) collective-permute-start(f32[2,32,10,1]{3,2,1,0:T(8,128)S(1)} %get-tuple-element.522), channel_id=1, source_target_pairs={{1,0},{2,1},{3,2},{4,3},{5,4},{6,5},{7,6},{8,7},{9,8},{10,9},{11,1... | collective-permute-start | bytes 7688 | tf_op jit(solution)/shard_map/ppermute | solution.py:20
  160.4 432.7 %collective-permute-start.3 = (f32[2,32,10,1]{3,2,1,0:T(8,128)}, f32[2,32,10,1]{3,2,1,0:T(8,128)S(1)}, u32[]{:S(2)}, u32[]{:S(2)}) collective-permute-start(f32[2,32,10,1]{3,2,1,0:T(8,128)} %get-tuple-element.521), channel_id=1, source_target_pairs={{0,1},{1,2},{2,3},{3,4},{4,5},{5,6},{6,7},{7,8},{8,9},{9,10},{10,1... | collective-permute-start | bytes 7688 | tf_op jit(solution)/shard_map/ppermute | solution.py:17
  167.1 426.0 %collective-permute-start.2 = (f32[2,32,10,1]{3,2,1,0:T(8,128)}, f32[2,32,10,1]{3,2,1,0:T(8,128)S(1)}, u32[]{:S(2)}, u32[]{:S(2)}) collective-permute-start(f32[2,32,10,1]{3,2,1,0:T(8,128)} %get-tuple-element.520), channel_id=1, source_target_pairs={{1,0},{2,1},{3,2},{4,3},{5,4},{6,5},{7,6},{8,7},{9,8},{10,9},{11,1... | collective-permute-start | bytes 7688 | tf_op jit(solution)/shard_map/ppermute | solution.py:20
  176.7 6.3 copy-start.40
  189.7 6.3 copy-start.40
  241.7 6.3 copy-start.40
  254.7 6.3 copy-start.40
  306.7 6.3 copy-start.40
  319.7 6.3 copy-start.40
  566.6 6.3 copy-start.40
  579.6 6.3 copy-start.40
  594.3 307.4 %collective-permute-start.8 = (f32[2,32,1,128]{3,2,1,0:T(1,128)S(1)}, f32[2,32,1,128]{3,2,1,0:T(1,128)S(1)}, u32[]{:S(2)}, u32[]{:S(2)}) collective-permute-start(f32[2,32,1,128]{3,2,1,0:T(1,128)S(1)} %get-tuple-element.531), channel_id=1, source_target_pairs={{32,0},{64,32},{96,64},{128,96},{160,128},{192,160},{224,192},{256... | collective-permute-start | bytes 98312 | tf_op jit(solution)/shard_map/ppermute | solution.py:20
  596.3 305.5 %collective-permute-start.9 = (f32[2,32,1,128]{3,2,1,0:T(1,128)S(1)}, f32[2,32,1,128]{3,2,1,0:T(1,128)S(1)}, u32[]{:S(2)}, u32[]{:S(2)}) collective-permute-start(f32[2,32,1,128]{3,2,1,0:T(1,128)S(1)} %get-tuple-element.530), channel_id=1, source_target_pairs={{0,32},{32,64},{64,96},{96,128},{128,160},{160,192},{192,224},{224... | collective-permute-start | bytes 98312 | tf_op jit(solution)/shard_map/ppermute | solution.py:17
  902.1 16.6 %collective-permute-start.11 = (f32[2,32,10,1]{3,2,1,0:T(8,128)S(1)}, f32[2,32,10,1]{3,2,1,0:T(8,128)S(1)}, u32[]{:S(2)}, u32[]{:S(2)}) collective-permute-start(f32[2,32,10,1]{3,2,1,0:T(8,128)S(1)} %get-tuple-element.519), channel_id=1, source_target_pairs={{0,1},{1,2},{2,3},{3,4},{4,5},{5,6},{6,7},{7,8},{8,9},{9,10},{10,1... | collective-permute-start | bytes 7688 | tf_op jit(solution)/shard_map/ppermute | solution.py:17
  907.4 14.8 %collective-permute-start.10 = (f32[2,32,10,1]{3,2,1,0:T(8,128)S(1)}, f32[2,32,10,1]{3,2,1,0:T(8,128)S(1)}, u32[]{:S(2)}, u32[]{:S(2)}) collective-permute-start(f32[2,32,10,1]{3,2,1,0:T(8,128)S(1)} %get-tuple-element.518), channel_id=1, source_target_pairs={{1,0},{2,1},{3,2},{4,3},{5,4},{6,5},{7,6},{8,7},{9,8},{10,9},{11,1... | collective-permute-start | bytes 7688 | tf_op jit(solution)/shard_map/ppermute | solution.py:20
  (687 other events, 922.5 us)
where the time goes:
time: 941 us; the launch traced here: 923 us
  local copies, waits for them, and re-layouts  316 us (34%)
  matrix products  209 us (22%)
  loops' own time  189 us (20%)
  blocking collectives  102 us (11%)
  other arithmetic  46.2 us (5%)
  starting transfers between devices  41.3 us (4%)
  waiting for transfers between devices  18.9 us (2%)
    while x1920, local copies, waits for them, and re-layouts  250 us
    another operation x2, loops' own time, backward_lines(): lax.scan(backward_one_line, running, jnp.arange(solid.shape[0], dtype=jnp...  125 us
    psum x1, blocking collectives, shards(): lax.psum((running[0], running[1], running[2], running[3], running[4], run...  102 us
    another operation x1, loops' own time, forward_coupling(): lax.map(forward_one_line, jnp.arange(solid.shape[0], dtype=jnp.int32))  64.3 us
    dynamic_slice x96, local copies, waits for them, and re-layouts, forward_coupling(): lax.map(forward_one_line, jnp.arange(solid.shape[0], dtype=jnp.int32))  55.9 us
    dot_general x64, matrix products, backprop(): jnp.dot(w_out, d_logits, preferred_element_type=jnp.float32)  39.4 us
    dot_general x64, matrix products, network(): jnp.dot(w_in.T, features, preferred_element_type=jnp.float32)  35.9 us
    dot_general x64, matrix products, backprop(): jnp.dot(w_mid, d_hidden_two, preferred_element_type=jnp.float32)  33.9 us
  transfers between devices with their start and end apart: 12, of which 3 were waited for; matrix products, arithmetic and copies ran while one was open for 44% of the time, Pallas kernels for 0%

commit v1 on v0

v1 whole, which is shorter than its diff:
```python
import functools
import math

import jax
import jax.numpy as jnp
from jax import lax
from jax.experimental import pallas as pl
from jax.experimental.pallas import tpu as pltpu
from jax.sharding import PartitionSpec as P

time_step = 0.15
loss_gain = 16.0
DESC, HID, XB, YB = 10, 64, 8, 128
ONES = DESC * XB + 2 * XB
KF = ONES + 16
WIDE = XB * HID
GROUP = 256
STREAMS = 4
BF, F32 = jnp.bfloat16, jnp.float32

VMEM = pl.BlockSpec(memory_space=pltpu.VMEM)
SMEM = pl.BlockSpec(memory_space=pltpu.SMEM)


def nn(a, b):
    return lax.dot_general(a, b, (((1,), (0,)), ((), ())), preferred_element_type=F32)


def nt(a, b):
    return lax.dot_general(a, b, (((1,), (1,)), ((), ())), preferred_element_type=F32)


def tn(a, b):
    return lax.dot_general(a, b, (((0,), (0,)), ((), ())), preferred_element_type=F32)


def lookup(material, table_ref):
    out = jnp.zeros(material.shape, F32)
    for kind in range(4):
        out = jnp.where(material == kind, table_ref[kind], out)
    return out


def iota(shape, dim):
    return lax.broadcasted_iota(jnp.int32, shape, dim)


def pack_columns(fields, depth, lo_ref, hi_ref):
    lane = iota((XB, YB), 1)

    def one(z, carry):
        lo, hi = carry
        for f, field in enumerate(fields):
            v = field(z)
            spot = f * depth + z
            lo = jnp.where(lane == spot, pltpu.roll(v, spot, 1), lo)
            hi = jnp.where(lane == spot, pltpu.roll(v, lax.rem(spot + 1, YB), 1), hi)
        return lo, hi

    zero = jnp.zeros((XB, YB), F32)
    lo, hi = lax.fori_loop(0, depth, one, (zero, zero), unroll=4)
    lo_ref[...] = lo
    hi_ref[...] = hi


def edges_kernel(
    solid, fluid, material, fixed, cond_s, cond_f, cot_s, cot_f,
    row_lo, row_hi, col_lo, col_hi, push,
):
    depth = solid.shape[0]
    weight = time_step * (1.0 - fixed[...].astype(F32))
    kind = material[...]
    push[0] = lookup(kind, cond_s) * (weight * cot_s[...])
    push[1] = lookup(kind, cond_f) * (weight * cot_f[...])
    views = (solid, fluid, push.at[0], push.at[1])
    for f, view in enumerate(views):
        row_lo[f] = view[:, 0, :]
        row_hi[f] = view[:, XB - 1, :]
    pack_columns([lambda z, view=view: view[z] for view in views], depth, col_lo, col_hi)


def spread_weights(w_in, b_in, w_mid, w_out, first_ref, mid_ref, out_ref):
    high = b_in.astype(BF)
    rest = b_in - high.astype(F32)
    middle = rest.astype(BF)
    low = (rest - middle.astype(F32)).astype(BF)
    stacked = jnp.concatenate(
        [w_in.astype(F32), high.astype(F32), middle.astype(F32), low.astype(F32), jnp.zeros((1, HID), F32)],
        axis=0,
    ).astype(BF)
    row, column = iota((16, KF), 0), iota((16, KF), 1)
    for x in range(XB):
        want = jnp.where(row < DESC + 2, row * XB + x, ONES + row - (DESC + 2))
        pick = (column == want).astype(F32).astype(BF)
        first_ref[x * HID : (x + 1) * HID, :] = tn(stacked, pick).astype(BF)
    lane = iota((HID, GROUP), 1)
    spot = iota((HID, GROUP), 0)
    for j in range(GROUP // HID):
        pick = (lane == spot + j * HID).astype(F32).astype(BF)
        if mid_ref is not None:
            mid_ref[0, j * HID : (j + 1) * HID, :] = tn(w_mid, pick).astype(BF)
            mid_ref[1, j * HID : (j + 1) * HID, :] = nn(w_mid, pick).astype(BF)
    spot = iota((HID, WIDE), 0)
    lane = iota((HID, WIDE), 1)
    pick = ((lane - spot) % HID == 0).astype(F32).astype(BF)
    spread = nn(w_out, pick)
    place = (iota((XB, WIDE), 1) // HID) == iota((XB, WIDE), 0)
    for k in range(spread.shape[0]):
        line = jnp.broadcast_to(spread[k : k + 1], (XB, WIDE))
        out_ref[k * XB : (k + 1) * XB, :] = jnp.where(place, line, 0.0).astype(BF)


def features_of(desc, solid, fluid, pair):
    sides = []
    for k in range(2):
        d = desc[:, 2 * pair + k].astype(F32).reshape(DESC * XB, YB)
        sides.append(
            jnp.concatenate([d, solid[k], fluid[k], jnp.ones((16, YB), F32)], axis=0).astype(BF)
        )
    return jnp.concatenate(sides, axis=1)


def blocks(value, size=GROUP):
    return [value[i * size : (i + 1) * size] for i in range(value.shape[0] // size)]


def lockstep(streams):
    alive = list(streams)
    while alive:
        alive = [stream for stream in alive if next(stream, alive) is not alive]


def forward(features, first, mid, out, bias_mid, bias_out):
    tops = [nn(first[g * GROUP : (g + 1) * GROUP], features) for g in range(WIDE // GROUP)]
    yield
    bias = jnp.concatenate([bias_mid[...]] * (GROUP // HID), axis=0)
    bias = jnp.concatenate([bias, bias], axis=1)
    h1, lower = [], []
    for top in tops:
        h1.append(jnp.tanh(top).astype(BF))
        lower.append(nn(mid[0], h1[-1]))
        yield
    h2 = []
    for top in lower:
        h2.append(jnp.tanh(top + bias).astype(BF))
        yield
    h1, h2 = jnp.concatenate(h1, axis=0), jnp.concatenate(h2, axis=0)
    logits = nn(out[...], h2)
    yield
    return h1, h2, logits[:XB] + bias_out[0], logits[XB:] + bias_out[1]


def softplus_terms(v):
    e = jnp.exp(-jnp.abs(v))
    plus = jnp.maximum(v, 0.0) + jnp.log1p(e)
    r = 1.0 / (1.0 + e)
    return plus, jnp.where(v >= 0, r, e * r)


def wide(pair):
    return jnp.concatenate([pair[0], pair[1]], axis=1)


def forward_kernel(
    desc, solid, fluid, w_in, b_in, w_mid, b_mid, w_out, b_out,
    h1_ref, h2_ref, logits_ref, first, mid, out, bias,
):
    spread_weights(w_in[...], b_in[...], w_mid[...], w_out[...], first, mid, out)
    eye = (iota((HID, HID), 0) == iota((HID, HID), 1)).astype(F32)
    column = jnp.sum(eye * b_mid[...], axis=1, keepdims=True)
    bias[...] = jnp.broadcast_to(column, (HID, YB))

    def stream(pair):
        s = [solid[2 * pair + k] for k in range(2)]
        f = [fluid[2 * pair + k] for k in range(2)]
        features = features_of(desc, s, f, pair)
        h1, h2, l0, l1 = yield from forward(features, first, mid, out, bias, b_out)
        h1_ref[pair] = h1
        h2_ref[pair] = h2
        logits_ref[pair, 0] = l0
        logits_ref[pair, 1] = l1

    def one(step, _):
        lockstep([stream(STREAMS * step + k) for k in range(STREAMS)])
        return 0

    lax.fori_loop(0, solid.shape[0] // 2 // STREAMS, one, 0)


def laplace(v, above, below, left, right):
    row, lane = iota((XB, YB), 0), iota((XB, YB), 1)
    down = jnp.where(row == XB - 1, below, pltpu.roll(v, XB - 1, 0))
    up = jnp.where(row == 0, above, pltpu.roll(v, 1, 0))
    east = jnp.where(lane == YB - 1, right, pltpu.roll(v, YB - 1, 1))
    west = jnp.where(lane == 0, left, pltpu.roll(v, 1, 1))
    return down + up + east + west - 4.0 * v


def rim(f, z, depth, rows_lo, rows_hi, cols_lo, cols_hi):
    spot = f * depth + z
    above = jnp.broadcast_to(rows_lo[f, pl.ds(z, 1), :], (XB, YB))
    below = jnp.broadcast_to(rows_hi[f, pl.ds(z, 1), :], (XB, YB))
    left = pltpu.roll(cols_lo[...], lax.rem(YB - spot, YB), 1)
    right = pltpu.roll(cols_hi[...], YB - 1 - spot, 1)
    return above, below, left, right


def backward(features, h1, h2, dl, mid, w_out_t, w_temps):
    tops = [nn(w_out_t[g * GROUP : (g + 1) * GROUP], dl) for g in range(WIDE // GROUP)]
    yield
    dh2, lower = [], []
    for top, h in zip(tops, blocks(h2)):
        h = h.astype(F32)
        dh2.append((top * (1.0 - h * h)).astype(BF))
        lower.append(nn(mid[1], dh2[-1]))
        yield
    dh1 = []
    for top, h in zip(lower, blocks(h1)):
        h = h.astype(F32)
        dh1.append((top * (1.0 - h * h)).astype(BF))
        yield
    dh1, dh2 = jnp.concatenate(dh1, axis=0), jnp.concatenate(dh2, axis=0)
    temps = nn(w_temps[...], dh1)
    one_rows = jnp.ones((16, 2 * YB), BF)
    left = jnp.concatenate(
        [jnp.concatenate([h1[x * HID : (x + 1) * HID], one_rows], axis=0) for x in range(XB)], axis=1
    )
    right = jnp.concatenate([dh2[x * HID : (x + 1) * HID] for x in range(XB)], axis=1)
    terms = nt(features, dh1), nt(left, right), nt(dl, h2)
    yield
    return temps, *terms


def steps_kernel(
    desc, solid, fluid, material, fixed, cond_s, cond_f, cot_s, cot_f, push,
    rows_lo, rows_hi, cols_lo, cols_hi,
    h1_ref, h2_ref, logits_ref, first, mid, out, bias, w_in_temps, b_out,
    part, later_push, row_lo, row_hi, col_lo, col_hi, payload,
    w_out_t, w_temps, acc_in, acc_mid, acc_out, acc_dl,
):
    depth = solid.shape[0]
    eye = (iota((2 * XB, 2 * XB), 0) == iota((2 * XB, 2 * XB), 1)).astype(F32).astype(BF)
    w_out_t[...] = tn(out[...], eye).astype(BF)
    pick = ((iota((HID, WIDE), 1) - iota((HID, WIDE), 0)) % HID == 0).astype(F32).astype(BF)
    spread = nn(w_in_temps[...], pick)
    place = (iota((XB, WIDE), 1) // HID) == iota((XB, WIDE), 0)
    for k in range(2):
        line = jnp.broadcast_to(spread[k : k + 1], (XB, WIDE))
        w_temps[k * XB : (k + 1) * XB, :] = jnp.where(place, line, 0.0).astype(BF)
    acc_in[...] = jnp.zeros_like(acc_in)
    acc_mid[...] = jnp.zeros_like(acc_mid)
    acc_out[...] = jnp.zeros_like(acc_out)
    acc_dl[...] = jnp.zeros_like(acc_dl)

    def stream(pair):
        zs = [2 * pair + k for k in range(2)]
        rims = (rows_lo, rows_hi, cols_lo, cols_hi)
        weight = [time_step * (1.0 - fixed[z].astype(F32)) for z in zs]
        k_s = [lookup(material[z], cond_s) for z in zs]
        k_f = [lookup(material[z], cond_f) for z in zs]
        s0 = [solid[z] for z in zs]
        f0 = [fluid[z] for z in zs]
        h_first, h_slope = softplus_terms(logits_ref[pair, 0])
        a_first, a_slope = softplus_terms(logits_ref[pair, 1])
        c0 = h_first * a_first
        lap_s = [laplace(s0[k], *rim(0, zs[k], depth, *rims)) for k in range(2)]
        lap_f = [laplace(f0[k], *rim(1, zs[k], depth, *rims)) for k in range(2)]
        weight, k_s, k_f = wide(weight), wide(k_s), wide(k_f)
        s0w, f0w = wide(s0), wide(f0)
        gap0 = f0w - s0w
        swing = c0 * gap0
        s1 = s0w + weight * (k_s * wide(lap_s) + swing)
        f1 = f0w + weight * (k_f * wide(lap_f) - swing)

        features1 = features_of(desc, (s1[:, :YB], s1[:, YB:]), (f1[:, :YB], f1[:, YB:]), pair)
        g1, g2, l0, l1 = yield from forward(features1, first, mid, out, bias, b_out)
        h_sf, h_sl = softplus_terms(l0)
        a_sf, a_sl = softplus_terms(l1)
        gs, gf = wide([cot_s[z] for z in zs]), wide([cot_f[z] for z in zs])
        us, uf = weight * gs, weight * gf
        dcoup = (f1 - s1) * (us - uf)
        dl = jnp.concatenate([dcoup * a_sf * h_sl, dcoup * h_sf * a_sl], axis=0).astype(BF)
        temps, t_in, t_mid, t_out = yield from backward(features1, g1, g2, dl, mid, w_out_t, w_temps)
        lap_s = wide([laplace(push[0, z], *rim(2, z, depth, *rims)) for z in zs])
        lap_f = wide([laplace(push[1, z], *rim(3, z, depth, *rims)) for z in zs])
        swing = h_sf * a_sf * (uf - us)
        gs = gs + lap_s + swing + temps[:XB]
        gf = gf + lap_f - swing + temps[XB:]

        us, uf = weight * gs, weight * gf
        ps, pf = k_s * us, k_f * uf
        dcoup = gap0 * (us - uf)
        dl0 = jnp.concatenate([dcoup * a_first * h_slope, dcoup * h_first * a_slope], axis=0).astype(BF)
        features0 = features_of(desc, s0, f0, pair)
        temps, u_in, u_mid, u_out = yield from backward(
            features0, h1_ref[pair], h2_ref[pair], dl0, mid, w_out_t, w_temps
        )
        swing = c0 * (uf - us)
        gs = gs + swing + temps[:XB]
        gf = gf - swing + temps[XB:]
        for k in range(2):
            lanes = slice(k * YB, (k + 1) * YB)
            part[0, zs[k]] = gs[:, lanes]
            part[1, zs[k]] = gf[:, lanes]
            later_push[0, zs[k]] = ps[:, lanes]
            later_push[1, zs[k]] = pf[:, lanes]
        acc_in[...] += t_in + u_in
        acc_mid[...] += t_mid + u_mid
        acc_out[...] += t_out + u_out
        acc_dl[...] += dl.astype(F32) + dl0.astype(F32)

    def one(step, _):
        lockstep([stream(STREAMS * step + k) for k in range(STREAMS)])
        return 0

    lax.fori_loop(0, depth // 2 // STREAMS, one, 0)

    for f in range(2):
        row_lo[f] = later_push[f, :, 0, :]
        row_hi[f] = later_push[f, :, XB - 1, :]
    pack_columns([lambda z, f=f: later_push[f, z] for f in range(2)], depth, col_lo, col_hi)

    def diagonal(acc, blocks):
        same = (iota((XB, WIDE), 1) // HID) == iota((XB, WIDE), 0)
        lines = []
        for b in range(blocks):
            kept = jnp.where(same, acc[b * XB : (b + 1) * XB, :], 0.0)
            lines.append(jnp.sum(kept, axis=0, keepdims=True))
        lines = jnp.concatenate(lines, axis=0)
        total = lines[:, :YB]
        for j in range(1, WIDE // YB):
            total = total + lines[:, j * YB : (j + 1) * YB]
        return total[:, :HID] + total[:, HID:]

    half = HID // 2
    payload[:half, :HID] = acc_mid[:half, :]
    payload[:half, HID:] = acc_mid[half:HID, :]
    payload[half:, :] = jnp.zeros((16, YB), F32)
    payload[half : half + 13, :HID] = diagonal(acc_in, 13)
    payload[half : half + 1, HID:] = acc_mid[HID : HID + 1, :]
    payload[half + 1 : half + 3, HID:] = diagonal(acc_out, 2)
    dl_rows = jnp.sum(acc_dl[...], axis=1, keepdims=True)
    for k in range(2):
        total = jnp.sum(dl_rows[k * XB : (k + 1) * XB], axis=0, keepdims=True)
        payload[half + 3 + k : half + 4 + k, HID:] = jnp.broadcast_to(total, (1, HID))


def finish_kernel(
    scale, part, push, rows_lo, rows_hi, cols_lo, cols_hi, summed,
    adj_s, adj_f, g_w_in, g_b_in, g_w_mid, g_b_mid, g_w_out, g_b_out,
):
    depth = part.shape[1]
    rims = (rows_lo, rows_hi, cols_lo, cols_hi)

    def one(z, _):
        for f, adj in enumerate((adj_s, adj_f)):
            adj[z] = part[f, z] + laplace(push[f, z], *rim(f, z, depth, *rims))
        return 0

    lax.fori_loop(0, depth, one, 0, unroll=4)
    half = HID // 2
    g_w_mid[:half, :] = summed[:half, :HID] * scale
    g_w_mid[half:, :] = summed[:half, HID:] * scale
    g_w_in[...] = summed[half : half + 12, :HID] * scale
    g_b_in[...] = summed[half + 12 : half + 13, :HID] * scale
    g_b_mid[...] = summed[half : half + 1, HID:] * scale
    g_w_out[...] = summed[half + 1 : half + 3, HID:] * scale
    g_b_out[...] = summed[half + 3 : half + 5, HID:] * scale


def shift(value, axis, step):
    count = lax.axis_size(axis)
    pairs = [(i, i + step) for i in range(count) if 0 <= i + step < count]
    return lax.ppermute(value, axis, pairs)


def exchange(row_lo, row_hi, col_lo, col_hi):
    return (
        shift(row_hi, "grp", 1),
        shift(row_lo, "grp", -1),
        shift(col_hi, "col", 1),
        shift(col_lo, "col", -1),
    )


def torus_groups():
    at = lambda x, y, z, core: (2 * z + y % 2) * 32 + 8 * x + 2 * (y // 2) + core
    xs, ys, zs, cores = range(4), range(8), range(8), range(2)
    return (
        [[at(x, y, z, c) for x in xs for c in cores] for y in ys for z in zs],
        [[at(x, y, z, c) for y in ys] for x in xs for z in zs for c in cores],
        [[at(x, y, z, c) for z in zs] for x in xs for y in ys for c in cores],
    )


def total_over_devices(value):
    axes = ("grp", "col")
    count = [lax.axis_size(axis) for axis in axes]
    groups = torus_groups() if count == [16, 32] else ([list(range(count[0] * count[1]))],)
    for members in groups:
        copies = jnp.broadcast_to(value[None], (len(members[0]), *value.shape))
        value = lax.all_to_all(copies, axes, 0, 0, axis_index_groups=members).sum(0)
    return value


def shape(dims, kind=F32):
    return jax.ShapeDtypeStruct(dims, kind)


def shards(
    descriptors, solid_temp, fluid_temp, material, fixed_mask, solid_cond, fluid_cond,
    w_in, b_in, w_mid, b_mid, w_out, b_out, solid_cot, fluid_cot,
):
    depth = solid_temp.shape[0]
    field = (depth, XB, YB)
    rows, column = (4, depth, YB), (XB, YB)
    *edges, push = pl.pallas_call(
        edges_kernel,
        out_shape=[shape(rows), shape(rows), shape(column), shape(column), shape((2,) + field)],
        in_specs=[VMEM] * 4 + [SMEM] * 2 + [VMEM] * 2,
        out_specs=[VMEM] * 5,
        name="edges",
    )(solid_temp, fluid_temp, material, fixed_mask, solid_cond, fluid_cond, solid_cot, fluid_cot)
    received = exchange(*edges)

    pairs = depth // 2
    kept = [
        shape((pairs, WIDE, 2 * YB), BF),
        shape((pairs, WIDE, 2 * YB), BF),
        shape((pairs, 2, XB, 2 * YB)),
        shape((WIDE, KF), BF),
        shape((2, GROUP, GROUP), BF),
        shape((2 * XB, WIDE), BF),
        shape((HID, YB)),
    ]
    saved = pl.pallas_call(
        forward_kernel,
        out_shape=kept,
        in_specs=[VMEM] * 8 + [SMEM],
        out_specs=[VMEM] * len(kept),
        cost_estimate=pl.CostEstimate(flops=2**29, bytes_accessed=2**24, transcendentals=2**22),
        name="forward",
    )(descriptors, solid_temp, fluid_temp, w_in, b_in[None], w_mid, b_mid[None], w_out.T, b_out)

    part, later_push, *edges, payload = pl.pallas_call(
        steps_kernel,
        out_shape=[
            shape((2,) + field),
            shape((2,) + field),
            shape((2, depth, YB)),
            shape((2, depth, YB)),
            shape(column),
            shape(column),
            shape((48, YB)),
        ],
        in_specs=[VMEM] * 5 + [SMEM] * 2 + [VMEM] * 15 + [SMEM],
        out_specs=[VMEM] * 7,
        scratch_shapes=[
            pltpu.VMEM((WIDE, 2 * XB), BF),
            pltpu.VMEM((2 * XB, WIDE), BF),
            pltpu.VMEM((KF, WIDE), F32),
            pltpu.VMEM((HID + 16, HID), F32),
            pltpu.VMEM((2 * XB, WIDE), F32),
            pltpu.VMEM((2 * XB, 2 * YB), F32),
        ],
        cost_estimate=pl.CostEstimate(flops=2**31, bytes_accessed=2**24, transcendentals=2**22),
        name="steps",
    )(
        descriptors, solid_temp, fluid_temp, material, fixed_mask, solid_cond, fluid_cond,
        solid_cot, fluid_cot, push, *received, *saved, w_in[DESC:], b_out,
    )
    received = exchange(*edges)
    summed = total_over_devices(payload)

    cells = solid_temp.size * lax.axis_size("grp") * lax.axis_size("col")
    scale = loss_gain / math.sqrt(cells)
    adj_s, adj_f, *grads = pl.pallas_call(
        functools.partial(finish_kernel, scale),
        out_shape=[
            shape(field), shape(field),
            shape((12, HID)), shape((1, HID)), shape((HID, HID)), shape((1, HID)),
            shape((2, HID)), shape((2, HID)),
        ],
        in_specs=[VMEM] * 7,
        out_specs=[VMEM] * 8,
        name="finish",
    )(part, later_push, *received, summed)
    return (
        adj_s, adj_f, grads[0], grads[1][0], grads[2], grads[3][0], grads[4].T, grads[5][:, 0],
    )


def solution(mesh):
    field, whole = P(None, "grp", "col"), P()
    placed = (
        (P(None, None, "grp", "col"),) + (field,) * 4 + (whole,) * 8 + (field,) * 2
    )
    return jax.shard_map(
        shards,
        mesh=mesh,
        in_specs=placed,
        out_specs=(field, field) + (whole,) * 6,
        check_vma=False,
    )
```

time: 941 us -> 114 us (0.12); the launches traced: 923 us -> 114 us
  local copies, waits for them, and re-layouts: 316 us -> 5.18 us
  matrix products: 209 us -> 0 us
  loops' own time: 189 us -> 0 us
  blocking collectives: 102 us -> 24 us
  other arithmetic: 46.2 us -> 0.66 us
  Pallas kernels: 0 us -> 37 us
  waiting for transfers between devices: 18.9 us -> 5.6 us
    while x1920 -> x0, local copies, waits for them, and re-layouts: 250 us -> none
    dot_general x640 -> x0, matrix products: 209 us -> none  [the longest x64 39.4 us: backprop(): jnp.dot(w_out, d_logits, preferred_element_type=jnp.float32)]
    another operation x3 -> x0, loops' own time: 189 us -> none  [the longest x2 125 us: backward_lines(): lax.scan(backward_one_line, running, jnp.arange(solid.shape[0], dtype=jnp...]
    psum x1 -> x0, blocking collectives: 102 us -> none  [shards(): lax.psum((running[0], running[1], running[2], running[3], running[4], run...]
    dynamic_slice x160 -> x0, local copies, waits for them, and re-layouts: 56.5 us -> none  [the longest x96 55.9 us: forward_coupling(): lax.map(forward_one_line, jnp.arange(solid.shape[0], dtype=jnp.int32))]
    pallas_call x0 -> x4, Pallas kernels: none -> 37 us  [the longest x1 23.4 us: shards(): pl.pallas_call(steps_kernel, out_shape=[shape((2,) + field), shape((2,) +...]
    all_to_all x0 -> x2, blocking collectives: none -> 24 us  [total_over_devices(): value = lax.all_to_all(copies, axes, 0, 0, axis_index_groups=members).sum(0)]
    reduce_sum x64 -> x3, other arithmetic: 24.2 us -> 0.66 us  [total_over_devices(): value = lax.all_to_all(copies, axes, 0, 0, axis_index_groups=members).sum(0)]
  transfers between devices with their start and end apart: 12 -> 9, of which waited for: 3 -> 1; matrix products, arithmetic and copies ran while one was open for 44% -> 2% of each run, Pallas kernels for 0% -> 7%
where the time goes in v1:
time: 114 us
  starting transfers between devices  40.5 us (36%)
  Pallas kernels  37 us (32%)
  blocking collectives  24 us (21%)
  waiting for transfers between devices  5.6 us (5%)
  local copies, waits for them, and re-layouts  5.18 us (5%)
    ppermute x8, starting transfers between devices, shift(): return lax.ppermute(value, axis, pairs)  28.8 us
    all_to_all x2, blocking collectives, total_over_devices(): value = lax.all_to_all(copies, axes, 0, 0, axis_index_groups=members).sum(0)  24 us
    pallas_call x1, Pallas kernels, shards(): pl.pallas_call(steps_kernel, out_shape=[shape((2,) + field), shape((2,) +...  23.4 us
    all_to_all x1, starting transfers between devices, total_over_devices(): value = lax.all_to_all(copies, axes, 0, 0, axis_index_groups=members).sum(0)  11.8 us
    pallas_call x1, Pallas kernels, shards(): pl.pallas_call(forward_kernel, out_shape=kept, in_specs=[VMEM] * 8 + [SME...  8.02 us
    ppermute x8, waiting for transfers between devices, shift(): return lax.ppermute(value, axis, pairs)  5.59 us
    pallas_call x1, Pallas kernels, shards(): pl.pallas_call(edges_kernel, out_shape=[shape(rows), shape(rows), shape(c...  2.99 us
    pallas_call x1, Pallas kernels, shards(): pl.pallas_call(functools.partial(finish_kernel, scale), out_shape=[shape(...  2.6 us
  transfers between devices with their start and end apart: 9, of which 1 were waited for; matrix products, arithmetic and copies ran while one was open for 2% of the time, Pallas kernels for 7%

profile of v1, /device:TPU:57, one launch (start us, length us, event | category | flops | bytes accessed | tf_op | source)
XLA Modules:
  0.0 113.8 jit_solution(10620074026767297923)
XLA Ops:
  0.6 3.0 %edges.1 = (f32[4,32,128]{2,1,0:T(8,128)}, f32[4,32,128]{2,1,0:T(8,128)}, f32[8,128]{1,0:T(8,128)}, f32[8,128]{1,0:T(8,128)}, f32[2,32,8,128]{3,2,1,0:T(8,128)}) custom-call(f32[32,8,128]{2,1,0:T(8,128)} %solid.5, f32[32,8,128]{2,1,0:T(8,128)} %fluid.5, s32[32,8,128]{2,1,0:T(8,128)} %material.3, s32[32,8,128]{2,1,0:T(8,128)} %fixed.3, f32[4]{0:T(128)} %cond_s.3, ...), custom_call_target="tpu_custom_call" | custom-call | tf_op jit(solution)/shard_map/edges/pallas_call | solution.py:417
  3.6 4.8 %collective-permute-start = (f32[4,32,128]{2,1,0:T(8,128)}, f32[4,32,128]{2,1,0:T(8,128)S(1)}, u32[]{:S(2)}, u32[]{:S(2)}) collective-permute-start(f32[4,32,128]{2,1,0:T(8,128)} %get-tuple-element.36), channel_id=1, source_target_pairs={{0,32},{32,64},{64,96},{96,128},{128,160},{160,192},{192,224},{224... | collective-permute-start | bytes 196616 | tf_op jit(solution)/shard_map/ppermute | solution.py:374
  8.4 1.9 %collective-permute-start.1 = (f32[4,32,128]{2,1,0:T(8,128)}, f32[4,32,128]{2,1,0:T(8,128)S(1)}, u32[]{:S(2)}, u32[]{:S(2)}) collective-permute-start(f32[4,32,128]{2,1,0:T(8,128)} %get-tuple-element.37), channel_id=1, source_target_pairs={{32,0},{64,32},{96,64},{128,96},{160,128},{192,160},{224,192},{256... | collective-permute-start | bytes 196616 | tf_op jit(solution)/shard_map/ppermute | solution.py:374
  10.3 3.3 %collective-permute-start.2 = (f32[8,128]{1,0:T(8,128)}, f32[8,128]{1,0:T(8,128)S(1)}, u32[]{:S(2)}, u32[]{:S(2)}) collective-permute-start(f32[8,128]{1,0:T(8,128)} %get-tuple-element.38), channel_id=1, source_target_pairs={{0,1},{1,2},{2,3},{3,4},{4,5},{5,6},{6,7},{7,8},{8,9},{9,10},{10,1... | collective-permute-start | bytes 12296 | tf_op jit(solution)/shard_map/ppermute | solution.py:374
  13.6 1.9 %collective-permute-start.3 = (f32[8,128]{1,0:T(8,128)}, f32[8,128]{1,0:T(8,128)S(1)}, u32[]{:S(2)}, u32[]{:S(2)}) collective-permute-start(f32[8,128]{1,0:T(8,128)} %get-tuple-element.39), channel_id=1, source_target_pairs={{1,0},{2,1},{3,2},{4,3},{5,4},{6,5},{7,6},{8,7},{9,8},{10,9},{11,1... | collective-permute-start | bytes 12296 | tf_op jit(solution)/shard_map/ppermute | solution.py:374
  15.5 8.0 %forward.1 = (bf16[16,512,256]{2,1,0:T(8,128)(2,1)}, bf16[16,512,256]{2,1,0:T(8,128)(2,1)}, f32[16,2,8,256]{3,2,1,0:T(8,128)}, bf16[512,112]{1,0:T(8,128)(2,1)},...) custom-call(bf16[10,32,8,128]{3,2,1,0:T(8,128)(2,1)} %desc.3, f32[32,8,128]{2,1,0:T(8,128)} %solid.5, ...), custom_call_target="tpu_custom_call" | custom-call | flops 536870912 | bytes 16777216 | tf_op jit(solution)/shard_map/forward/pallas_call | solution.py:436
  23.6 1.2 %slice.6.w_in_temps = bf16[2,64]{1,0:T(2,128)(2,1)} slice(bf16[12,64]{1,0:T(8,128)(2,1)} %w_in.1), slice={[10:12], [0:64]} | slice | bytes 512 | tf_op jit(solution)/shard_map/slice | solution.py:470
  24.8 0.5 copy-done.4
  25.4 0.1 copy-done
  25.5 23.4 %steps.1 = (f32[2,32,8,128]{3,2,1,0:T(8,128)}, f32[2,32,8,128]{3,2,1,0:T(8,128)}, f32[2,32,128]{2,1,0:T(8,128)}, f32[2,32,128]{2,1,0:T(8,128)}, f32[8,128]{1,0:T...) custom-call(bf16[10,32,8,128]{3,2,1,0:T(8,128)(2,1)} %desc.3, f32[32,8,128]{2,1,0:T(8,128)} %solid.5, f32[32,8,128]{2,1,0:T(8,128)} %fluid.5, ...), custom_call_target="tpu_custom_call" | custom-call | flops 2147483648 | bytes 16777216 | tf_op jit(solution)/shard_map/steps/pallas_call | solution.py:445
  48.9 0.8 broadcast_in_dim.12
  49.6 12.2 %all_to_all.15 = f32[8,48,128]{2,1,0:T(8,128)S(1)} all-to-all(f32[8,48,128]{2,1,0:T(8,128)S(1)} %broadcast_in_dim.12), channel_id=1, replica_groups={{0,1,8,9,16,17,24,25},{64,65,72,73,80,81,88,89},{128,129,136,137,144,14..., dimensions={0} | all-to-all | bytes 393216 | tf_op jit(solution)/shard_map/all_to_all | solution.py:402
  61.8 11.8 %all_to_all.16 = f32[8,48,128]{2,1,0:T(8,128)S(1)} all-to-all(f32[8,48,128]{2,1,0:T(8,128)S(1)} %broadcast_in_dim.13), channel_id=1, replica_groups={{0,32,2,34,4,36,6,38},{1,33,3,35,5,37,7,39},{64,96,66,98,68,100,70,102}..., dimensions={0} | all-to-all | bytes 393216 | tf_op jit(solution)/shard_map/all_to_all | solution.py:402
  73.7 0.7 broadcast_in_dim.28
  74.4 11.8 %all-to-all-start.2 = ((f32[8,48,128]{2,1,0:T(8,128)}), f32[8,48,128]{2,1,0:T(8,128)S(1)}, u32[]{:S(2)}, u32[]{:S(2)}) async-start(f32[8,48,128]{2,1,0:T(8,128)} %broadcast_in_dim.28), calls=%async_computation.2 | async-start | bytes 393216 | tf_op jit(solution)/shard_map/all_to_all | solution.py:402
  86.1 5.5 %collective-permute-start.4 = (f32[2,32,128]{2,1,0:T(8,128)}, f32[2,32,128]{2,1,0:T(8,128)S(1)}, u32[]{:S(2)}, u32[]{:S(2)}) collective-permute-start(f32[2,32,128]{2,1,0:T(8,128)} %get-tuple-element.49), channel_id=1, source_target_pairs={{0,32},{32,64},{64,96},{96,128},{128,160},{160,192},{192,224},{224... | collective-permute-start | bytes 98312 | tf_op jit(solution)/shard_map/ppermute | solution.py:374
  91.6 1.9 %collective-permute-start.5 = (f32[2,32,128]{2,1,0:T(8,128)}, f32[2,32,128]{2,1,0:T(8,128)S(1)}, u32[]{:S(2)}, u32[]{:S(2)}) collective-permute-start(f32[2,32,128]{2,1,0:T(8,128)} %get-tuple-element.50), channel_id=1, source_target_pairs={{32,0},{64,32},{96,64},{128,96},{160,128},{192,160},{224,192},{256... | collective-permute-start | bytes 98312 | tf_op jit(solution)/shard_map/ppermute | solution.py:374
  93.6 7.5 %collective-permute-start.6 = (f32[8,128]{1,0:T(8,128)}, f32[8,128]{1,0:T(8,128)S(1)}, u32[]{:S(2)}, u32[]{:S(2)}) collective-permute-start(f32[8,128]{1,0:T(8,128)} %get-tuple-element.51), channel_id=1, source_target_pairs={{0,1},{1,2},{2,3},{3,4},{4,5},{5,6},{6,7},{7,8},{8,9},{9,10},{10,1... | collective-permute-start | bytes 12296 | tf_op jit(solution)/shard_map/ppermute | solution.py:374
  101.1 1.9 %collective-permute-start.7 = (f32[8,128]{1,0:T(8,128)}, f32[8,128]{1,0:T(8,128)S(1)}, u32[]{:S(2)}, u32[]{:S(2)}) collective-permute-start(f32[8,128]{1,0:T(8,128)} %get-tuple-element.52), channel_id=1, source_target_pairs={{1,0},{2,1},{3,2},{4,3},{5,4},{6,5},{7,6},{8,7},{9,8},{10,9},{11,1... | collective-permute-start | bytes 12296 | tf_op jit(solution)/shard_map/ppermute | solution.py:374
  103.0 0.6 reduce_sum.29.summed
  103.7 5.6 %collective-permute-done.7.cols_hi = f32[8,128]{1,0:T(8,128)S(1)} collective-permute-done((f32[8,128]{1,0:T(8,128)}, f32[8,128]{1,0:T(8,128)S(1)}, u32[]{:S(2)}, u32[]{:S(2)}) %collective-permute-start.7) | collective-permute-done | bytes 4128 | tf_op jit(solution)/shard_map/ppermute | solution.py:374
  109.3 0.6 copy-done.7
  109.9 2.6 %finish.1 = (f32[32,8,128]{2,1,0:T(8,128)}, f32[32,8,128]{2,1,0:T(8,128)}, f32[12,64]{1,0:T(8,128)}, f32[1,64]{1,0:T(1,128)}, f32[64,64]{1,0:T(8,128)}, /*index=...) custom-call(f32[2,32,8,128]{3,2,1,0:T(8,128)} %get-tuple-element.47.part, f32[2,32,8,128]{3,2,1,0:T(8,128)} %get-tuple-element.48.push, ...), custom_call_target="tpu_custom_call" | custom-call | tf_op jit(solution)/shard_map/finish/pallas_call | solution.py:477
  112.5 1.3 %slice_reduce_fusion = f32[2]{0:T(128)} fusion(f32[2,64]{1,0:T(2,128)} %get-tuple-element.61), kind=kLoop, calls=%fused_computation | loop fusion | bytes 16 | tf_op jit(solution)/shard_map/slice | solution.py:489
  (24 shorter events, 0.2 us)
Async XLA Ops:
  3.6 21.2 %collective-permute-start = (f32[4,32,128]{2,1,0:T(8,128)}, f32[4,32,128]{2,1,0:T(8,128)S(1)}, u32[]{:S(2)}, u32[]{:S(2)}) collective-permute-start(f32[4,32,128]{2,1,0:T(8,128)} %get-tuple-element.36), channel_id=1, source_target_pairs={{0,32},{32,64},{64,96},{96,128},{128,160},{160,192},{192,224},{224... | collective-permute-start | bytes 196616 | tf_op jit(solution)/shard_map/ppermute | solution.py:374
  8.4 16.4 %collective-permute-start.1 = (f32[4,32,128]{2,1,0:T(8,128)}, f32[4,32,128]{2,1,0:T(8,128)S(1)}, u32[]{:S(2)}, u32[]{:S(2)}) collective-permute-start(f32[4,32,128]{2,1,0:T(8,128)} %get-tuple-element.37), channel_id=1, source_target_pairs={{32,0},{64,32},{96,64},{128,96},{160,128},{192,160},{224,192},{256... | collective-permute-start | bytes 196616 | tf_op jit(solution)/shard_map/ppermute | solution.py:374
  10.3 14.4 %collective-permute-start.2 = (f32[8,128]{1,0:T(8,128)}, f32[8,128]{1,0:T(8,128)S(1)}, u32[]{:S(2)}, u32[]{:S(2)}) collective-permute-start(f32[8,128]{1,0:T(8,128)} %get-tuple-element.38), channel_id=1, source_target_pairs={{0,1},{1,2},{2,3},{3,4},{4,5},{5,6},{6,7},{7,8},{8,9},{9,10},{10,1... | collective-permute-start | bytes 12296 | tf_op jit(solution)/shard_map/ppermute | solution.py:374
  13.6 11.2 %collective-permute-start.3 = (f32[8,128]{1,0:T(8,128)}, f32[8,128]{1,0:T(8,128)S(1)}, u32[]{:S(2)}, u32[]{:S(2)}) collective-permute-start(f32[8,128]{1,0:T(8,128)} %get-tuple-element.39), channel_id=1, source_target_pairs={{1,0},{2,1},{3,2},{4,3},{5,4},{6,5},{7,6},{8,7},{9,8},{10,9},{11,1... | collective-permute-start | bytes 12296 | tf_op jit(solution)/shard_map/ppermute | solution.py:374
  24.8 0.6 copy-start.4
  24.8 0.6 copy-start.5
  24.8 0.6 copy-start
  24.8 0.6 copy-start.1
  74.4 28.7 %all-to-all-start.2 = ((f32[8,48,128]{2,1,0:T(8,128)}), f32[8,48,128]{2,1,0:T(8,128)S(1)}, u32[]{:S(2)}, u32[]{:S(2)}) async-start(f32[8,48,128]{2,1,0:T(8,128)} %broadcast_in_dim.28), calls=%async_computation.2 | async-start | bytes 393216 | tf_op jit(solution)/shard_map/all_to_all | solution.py:402
  86.1 23.1 %collective-permute-start.4 = (f32[2,32,128]{2,1,0:T(8,128)}, f32[2,32,128]{2,1,0:T(8,128)S(1)}, u32[]{:S(2)}, u32[]{:S(2)}) collective-permute-start(f32[2,32,128]{2,1,0:T(8,128)} %get-tuple-element.49), channel_id=1, source_target_pairs={{0,32},{32,64},{64,96},{96,128},{128,160},{160,192},{192,224},{224... | collective-permute-start | bytes 98312 | tf_op jit(solution)/shard_map/ppermute | solution.py:374
  91.6 17.6 %collective-permute-start.5 = (f32[2,32,128]{2,1,0:T(8,128)}, f32[2,32,128]{2,1,0:T(8,128)S(1)}, u32[]{:S(2)}, u32[]{:S(2)}) collective-permute-start(f32[2,32,128]{2,1,0:T(8,128)} %get-tuple-element.50), channel_id=1, source_target_pairs={{32,0},{64,32},{96,64},{128,96},{160,128},{192,160},{224,192},{256... | collective-permute-start | bytes 98312 | tf_op jit(solution)/shard_map/ppermute | solution.py:374
  93.6 10.1 %collective-permute-start.6 = (f32[8,128]{1,0:T(8,128)}, f32[8,128]{1,0:T(8,128)S(1)}, u32[]{:S(2)}, u32[]{:S(2)}) collective-permute-start(f32[8,128]{1,0:T(8,128)} %get-tuple-element.51), channel_id=1, source_target_pairs={{0,1},{1,2},{2,3},{3,4},{4,5},{5,6},{6,7},{7,8},{8,9},{9,10},{10,1... | collective-permute-start | bytes 12296 | tf_op jit(solution)/shard_map/ppermute | solution.py:374
  101.1 8.1 %collective-permute-start.7 = (f32[8,128]{1,0:T(8,128)}, f32[8,128]{1,0:T(8,128)S(1)}, u32[]{:S(2)}, u32[]{:S(2)}) collective-permute-start(f32[8,128]{1,0:T(8,128)} %get-tuple-element.52), channel_id=1, source_target_pairs={{1,0},{2,1},{3,2},{4,3},{5,4},{6,5},{7,6},{8,7},{9,8},{10,9},{11,1... | collective-permute-start | bytes 12296 | tf_op jit(solution)/shard_map/ppermute | solution.py:374
  103.7 5.6 %copy-start.6 = (f32[8,128]{1,0:T(8,128)}, f32[8,128]{1,0:T(8,128)S(1)}, u32[]{:S(2)}) copy-start(f32[8,128]{1,0:T(8,128)S(1)} %collective-permute-done.6.cols_lo) | copy-start | bytes 12292
  109.2 0.6 copy-start.7
  109.2 0.6 copy-start.2
  109.3 0.6 copy-start.3

commit v2 on v1

--- a/solution.py
+++ b/solution.py
@@ -10,16 +10,18 @@
 
 time_step = 0.15
 loss_gain = 16.0
+LOADED = 12
 DESC, HID, XB, YB = 10, 64, 8, 128
 ONES = DESC * XB + 2 * XB
 KF = ONES + 16
 WIDE = XB * HID
 GROUP = 256
-STREAMS = 4
+STREAMS = 8
 BF, F32 = jnp.bfloat16, jnp.float32
 
 VMEM = pl.BlockSpec(memory_space=pltpu.VMEM)
 SMEM = pl.BlockSpec(memory_space=pltpu.SMEM)
+HBM = pl.BlockSpec(memory_space=pltpu.HBM)
 
 
 def nn(a, b):
@@ -63,10 +65,15 @@
     hi_ref[...] = hi
 
 
-def edges_kernel(
-    solid, fluid, material, fixed, cond_s, cond_f, cot_s, cot_f,
-    row_lo, row_hi, col_lo, col_hi, push,
-):
+def edges_kernel(cond_s, cond_f, *refs):
+    far, near, sems = refs[:LOADED], refs[LOADED : 2 * LOADED], refs[-1]
+    row_lo, row_hi, col_lo, col_hi, push = refs[2 * LOADED : -1]
+    copies = [pltpu.make_async_copy(far[i], near[i], sems.at[i]) for i in range(LOADED)]
+    for copy in copies:
+        copy.start()
+    for copy in copies[:6]:
+        copy.wait()
+    solid, fluid, material, fixed, cot_s, cot_f = near[:6]
     depth = solid.shape[0]
     weight = time_step * (1.0 - fixed[...].astype(F32))
     kind = material[...]
@@ -77,6 +84,8 @@
         row_lo[f] = view[:, 0, :]
         row_hi[f] = view[:, XB - 1, :]
     pack_columns([lambda z, view=view: view[z] for view in views], depth, col_lo, col_hi)
+    for copy in copies[6:]:
+        copy.wait()
 
 
 def spread_weights(w_in, b_in, w_mid, w_out, first_ref, mid_ref, out_ref):
@@ -234,7 +243,7 @@
 def steps_kernel(
     desc, solid, fluid, material, fixed, cond_s, cond_f, cot_s, cot_f, push,
     rows_lo, rows_hi, cols_lo, cols_hi,
-    h1_ref, h2_ref, logits_ref, first, mid, out, bias, w_in_temps, b_out,
+    h1_ref, h2_ref, logits_ref, first, mid, out, bias, w_in, b_out,
     part, later_push, row_lo, row_hi, col_lo, col_hi, payload,
     w_out_t, w_temps, acc_in, acc_mid, acc_out, acc_dl,
 ):
@@ -242,7 +251,7 @@
     eye = (iota((2 * XB, 2 * XB), 0) == iota((2 * XB, 2 * XB), 1)).astype(F32).astype(BF)
     w_out_t[...] = tn(out[...], eye).astype(BF)
     pick = ((iota((HID, WIDE), 1) - iota((HID, WIDE), 0)) % HID == 0).astype(F32).astype(BF)
-    spread = nn(w_in_temps[...], pick)
+    spread = nn(w_in[...].astype(F32)[DESC:].astype(BF), pick)
     place = (iota((XB, WIDE), 1) // HID) == iota((XB, WIDE), 0)
     for k in range(2):
         line = jnp.broadcast_to(spread[k : k + 1], (XB, WIDE))
@@ -333,16 +342,19 @@
         return total[:, :HID] + total[:, HID:]
 
     half = HID // 2
-    payload[:half, :HID] = acc_mid[:half, :]
-    payload[:half, HID:] = acc_mid[half:HID, :]
-    payload[half:, :] = jnp.zeros((16, YB), F32)
-    payload[half : half + 13, :HID] = diagonal(acc_in, 13)
-    payload[half : half + 1, HID:] = acc_mid[HID : HID + 1, :]
-    payload[half + 1 : half + 3, HID:] = diagonal(acc_out, 2)
+    grads = payload.at[0]
+    grads[:half, :HID] = acc_mid[:half, :]
+    grads[:half, HID:] = acc_mid[half:HID, :]
+    grads[half:, :] = jnp.zeros((16, YB), F32)
+    grads[half : half + 13, :HID] = diagonal(acc_in, 13)
+    grads[half : half + 1, HID:] = acc_mid[HID : HID + 1, :]
+    grads[half + 1 : half + 3, HID:] = diagonal(acc_out, 2)
     dl_rows = jnp.sum(acc_dl[...], axis=1, keepdims=True)
     for k in range(2):
         total = jnp.sum(dl_rows[k * XB : (k + 1) * XB], axis=0, keepdims=True)
-        payload[half + 3 + k : half + 4 + k, HID:] = jnp.broadcast_to(total, (1, HID))
+        grads[half + 3 + k : half + 4 + k, HID:] = jnp.broadcast_to(total, (1, HID))
+    for copy in range(1, payload.shape[0]):
+        payload[copy] = payload[0]
 
 
 def finish_kernel(
@@ -365,7 +377,9 @@
     g_b_in[...] = summed[half + 12 : half + 13, :HID] * scale
     g_b_mid[...] = summed[half : half + 1, HID:] * scale
     g_w_out[...] = summed[half + 1 : half + 3, HID:] * scale
-    g_b_out[...] = summed[half + 3 : half + 5, HID:] * scale
+    first = iota((1, HID), 1) == 0
+    for k in range(2):
+        g_b_out[k] = jnp.sum(jnp.where(first, summed[half + 3 + k : half + 4 + k, HID:], 0.0)) * scale
 
 
 def shift(value, axis, step):
@@ -393,14 +407,18 @@
     )
 
 
-def total_over_devices(value):
+def rings():
+    count = lax.axis_size("grp"), lax.axis_size("col")
+    return torus_groups() if count == (16, 32) else ([list(range(count[0] * count[1]))],)
+
+
+def total_over_devices(copies):
     axes = ("grp", "col")
-    count = [lax.axis_size(axis) for axis in axes]
-    groups = torus_groups() if count == [16, 32] else ([list(range(count[0] * count[1]))],)
-    for members in groups:
-        copies = jnp.broadcast_to(value[None], (len(members[0]), *value.shape))
-        value = lax.all_to_all(copies, axes, 0, 0, axis_index_groups=members).sum(0)
-    return value
+    for members in rings():
+        if copies.ndim == 2:
+            copies = jnp.broadcast_to(copies[None], (len(members[0]), *copies.shape))
+        copies = lax.all_to_all(copies, axes, 0, 0, axis_index_groups=members).sum(0)
+    return copies
 
 
 def shape(dims, kind=F32):
@@ -414,24 +432,33 @@
     depth = solid_temp.shape[0]
     field = (depth, XB, YB)
     rows, column = (4, depth, YB), (XB, YB)
-    *edges, push = pl.pallas_call(
+    given = (
+        solid_temp, fluid_temp, material, fixed_mask, solid_cot, fluid_cot,
+        descriptors, w_in, b_in[None], w_mid, b_mid[None], w_out.T,
+    )
+    *loaded, row_lo, row_hi, col_lo, col_hi, push = pl.pallas_call(
         edges_kernel,
-        out_shape=[shape(rows), shape(rows), shape(column), shape(column), shape((2,) + field)],
-        in_specs=[VMEM] * 4 + [SMEM] * 2 + [VMEM] * 2,
-        out_specs=[VMEM] * 5,
+        out_shape=[pltpu.VMEM(v.shape, v.dtype) for v in given]
+        + [shape(rows), shape(rows), shape(column), shape(column), pltpu.VMEM((2,) + field, F32)],
+        in_specs=[SMEM] * 2 + [HBM] * LOADED,
+        out_specs=[VMEM] * (LOADED + 5),
+        scratch_shapes=[pltpu.SemaphoreType.DMA((LOADED,))],
+        compiler_params=pltpu.CompilerParams(vmem_limit_bytes=65_050_000),
         name="edges",
-    )(solid_temp, fluid_temp, material, fixed_mask, solid_cond, fluid_cond, solid_cot, fluid_cot)
+    )(solid_cond, fluid_cond, *given)
+    edges = row_lo, row_hi, col_lo, col_hi
+    solid, fluid, material, fixed, cot_s, cot_f, desc, *weights = loaded
     received = exchange(*edges)
 
     pairs = depth // 2
     kept = [
-        shape((pairs, WIDE, 2 * YB), BF),
-        shape((pairs, WIDE, 2 * YB), BF),
-        shape((pairs, 2, XB, 2 * YB)),
-        shape((WIDE, KF), BF),
-        shape((2, GROUP, GROUP), BF),
-        shape((2 * XB, WIDE), BF),
-        shape((HID, YB)),
+        pltpu.VMEM((pairs, WIDE, 2 * YB), BF),
+        pltpu.VMEM((pairs, WIDE, 2 * YB), BF),
+        pltpu.VMEM((pairs, 2, XB, 2 * YB), F32),
+        pltpu.VMEM((WIDE, KF), BF),
+        pltpu.VMEM((2, GROUP, GROUP), BF),
+        pltpu.VMEM((2 * XB, WIDE), BF),
+        pltpu.VMEM((HID, YB), F32),
     ]
     saved = pl.pallas_call(
         forward_kernel,
@@ -440,7 +467,8 @@
         out_specs=[VMEM] * len(kept),
         cost_estimate=pl.CostEstimate(flops=2**29, bytes_accessed=2**24, transcendentals=2**22),
         name="forward",
-    )(descriptors, solid_temp, fluid_temp, w_in, b_in[None], w_mid, b_mid[None], w_out.T, b_out)
+        compiler_params=pltpu.CompilerParams(vmem_limit_bytes=24 * 2**20),
+    )(desc, solid, fluid, *weights, b_out)
 
     part, later_push, *edges, payload = pl.pallas_call(
         steps_kernel,
@@ -451,7 +479,7 @@
             shape((2, depth, YB)),
             shape(column),
             shape(column),
-            shape((48, YB)),
+            shape((len(rings()[0][0]), 48, YB)),
         ],
         in_specs=[VMEM] * 5 + [SMEM] * 2 + [VMEM] * 15 + [SMEM],
         out_specs=[VMEM] * 7,
@@ -465,9 +493,10 @@
         ],
         cost_estimate=pl.CostEstimate(flops=2**31, bytes_accessed=2**24, transcendentals=2**22),
         name="steps",
+        compiler_params=pltpu.CompilerParams(vmem_limit_bytes=32 * 2**20),
     )(
-        descriptors, solid_temp, fluid_temp, material, fixed_mask, solid_cond, fluid_cond,
-        solid_cot, fluid_cot, push, *received, *saved, w_in[DESC:], b_out,
+        desc, solid, fluid, material, fixed, solid_cond, fluid_cond,
+        cot_s, cot_f, push, *received, *saved, weights[0], b_out,
     )
     received = exchange(*edges)
     summed = total_over_devices(payload)
@@ -479,14 +508,15 @@
         out_shape=[
             shape(field), shape(field),
             shape((12, HID)), shape((1, HID)), shape((HID, HID)), shape((1, HID)),
-            shape((2, HID)), shape((2, HID)),
+            shape((2, HID)), shape((2,)),
         ],
         in_specs=[VMEM] * 7,
-        out_specs=[VMEM] * 8,
+        out_specs=[VMEM] * 7 + [SMEM],
         name="finish",
+        compiler_params=pltpu.CompilerParams(vmem_limit_bytes=16 * 2**20),
     )(part, later_push, *received, summed)
     return (
-        adj_s, adj_f, grads[0], grads[1][0], grads[2], grads[3][0], grads[4].T, grads[5][:, 0],
+        adj_s, adj_f, grads[0], grads[1][0], grads[2], grads[3][0], grads[4].T, grads[5],
     )
 
 

time: 114 us -> 101 us (0.89)
  Pallas kernels: 37 us -> 27.8 us
  local copies, waits for them, and re-layouts: 5.18 us -> 1.36 us
  waiting for transfers between devices: 5.6 us -> 7.64 us
  blocking collectives: 24 us -> 22.4 us
    pallas_call x1, Pallas kernels: 23.4 us -> 18.5 us  [shards(): pl.pallas_call(steps_kernel, out_shape=[shape((2,) + field), shape((2,) +...]
    pallas_call x1, Pallas kernels: 8.02 us -> 3.89 us  [shards(): pl.pallas_call(forward_kernel, out_shape=kept, in_specs=[VMEM] * 8 + [SME...]
    slice x2 -> x0, local copies, waits for them, and re-layouts: 2.48 us -> none  [the longest x1 1.29 us: shards(): grads[5][:, 0]]
    ppermute x8, waiting for transfers between devices: 5.59 us -> 7.64 us  [shift(): return lax.ppermute(value, axis, pairs)]
    all_to_all x2, blocking collectives: 24 us -> 22.4 us  [total_over_devices(): lax.all_to_all(copies, axes, 0, 0, axis_index_groups=members).sum(0)]
  transfers between devices with their start and end apart: 9 -> 9, of which waited for: 1 -> 2; matrix products, arithmetic and copies ran while one was open for 2% -> 0% of each run, Pallas kernels for 7% -> 4%
where the time goes in v2:
time: 101 us
  starting transfers between devices  40.5 us (40%)
  Pallas kernels  27.8 us (28%)
  blocking collectives  22.4 us (22%)
  waiting for transfers between devices  7.64 us (8%)
  local copies, waits for them, and re-layouts  1.36 us (1%)
    ppermute x8, starting transfers between devices, shift(): return lax.ppermute(value, axis, pairs)  28.8 us
    all_to_all x2, blocking collectives, total_over_devices(): lax.all_to_all(copies, axes, 0, 0, axis_index_groups=members).sum(0)  22.4 us
    pallas_call x1, Pallas kernels, shards(): pl.pallas_call(steps_kernel, out_shape=[shape((2,) + field), shape((2,) +...  18.5 us
    all_to_all x1, starting transfers between devices, total_over_devices(): lax.all_to_all(copies, axes, 0, 0, axis_index_groups=members).sum(0)  11.7 us
    ppermute x8, waiting for transfers between devices, shift(): return lax.ppermute(value, axis, pairs)  7.64 us
    pallas_call x1, Pallas kernels, shards(): pl.pallas_call(forward_kernel, out_shape=kept, in_specs=[VMEM] * 8 + [SME...  3.89 us
    pallas_call x1, Pallas kernels, shards(): pl.pallas_call(edges_kernel, out_shape=[pltpu.VMEM(v.shape, v.dtype) for...  3.74 us
  transfers between devices with their start and end apart: 9, of which 2 were waited for; matrix products, arithmetic and copies ran while one was open for 0% of the time, Pallas kernels for 4%

profile of v2, /device:TPU:57, one launch (start us, length us, event | category | flops | bytes accessed | tf_op | source)
XLA Modules:
  0.0 100.5 jit_solution(12975650576743368366)
XLA Ops:
  0.6 3.7 %edges.1 = (f32[32,8,128]{2,1,0:T(8,128)S(1)}, f32[32,8,128]{2,1,0:T(8,128)S(1)}, s32[32,8,128]{2,1,0:T(8,128)S(1)}, s32[32,8,128]{2,1,0:T(8,128)S(1)}, f32[32,8...) custom-call(f32[4]{0:T(128)} %cond_s.3, f32[4]{0:T(128)} %cond_f.3, ...), custom_call_target="tpu_custom_call" | custom-call | tf_op jit(solution)/shard_map/edges/pallas_call | solution.py:439
  4.4 0.0 copy-start
  4.4 0.0 copy-start.1
  4.4 4.8 %collective-permute-start = (f32[4,32,128]{2,1,0:T(8,128)}, f32[4,32,128]{2,1,0:T(8,128)S(1)}, u32[]{:S(2)}, u32[]{:S(2)}) collective-permute-start(f32[4,32,128]{2,1,0:T(8,128)} %get-tuple-element.55), channel_id=1, source_target_pairs={{0,32},{32,64},{64,96},{96,128},{128,160},{160,192},{192,224},{224... | collective-permute-start | bytes 196616 | tf_op jit(solution)/shard_map/ppermute | solution.py:388
  9.2 1.9 %collective-permute-start.1 = (f32[4,32,128]{2,1,0:T(8,128)}, f32[4,32,128]{2,1,0:T(8,128)S(1)}, u32[]{:S(2)}, u32[]{:S(2)}) collective-permute-start(f32[4,32,128]{2,1,0:T(8,128)} %get-tuple-element.56), channel_id=1, source_target_pairs={{32,0},{64,32},{96,64},{128,96},{160,128},{192,160},{224,192},{256... | collective-permute-start | bytes 196616 | tf_op jit(solution)/shard_map/ppermute | solution.py:388
  11.1 3.3 %collective-permute-start.2 = (f32[8,128]{1,0:T(8,128)}, f32[8,128]{1,0:T(8,128)S(1)}, u32[]{:S(2)}, u32[]{:S(2)}) collective-permute-start(f32[8,128]{1,0:T(8,128)} %get-tuple-element.57), channel_id=1, source_target_pairs={{0,1},{1,2},{2,3},{3,4},{4,5},{5,6},{6,7},{7,8},{8,9},{9,10},{10,1... | collective-permute-start | bytes 12296 | tf_op jit(solution)/shard_map/ppermute | solution.py:388
  14.4 1.9 %collective-permute-start.3 = (f32[8,128]{1,0:T(8,128)}, f32[8,128]{1,0:T(8,128)S(1)}, u32[]{:S(2)}, u32[]{:S(2)}) collective-permute-start(f32[8,128]{1,0:T(8,128)} %get-tuple-element.58), channel_id=1, source_target_pairs={{1,0},{2,1},{3,2},{4,3},{5,4},{6,5},{7,6},{8,7},{9,8},{10,9},{11,1... | collective-permute-start | bytes 12296 | tf_op jit(solution)/shard_map/ppermute | solution.py:388
  16.3 0.0 copy-start.2
  16.4 0.6 copy-done.2
  17.0 3.9 %forward.1 = (bf16[16,512,256]{2,1,0:T(8,128)(2,1)S(1)}, bf16[16,512,256]{2,1,0:T(8,128)(2,1)S(1)}, f32[16,2,8,256]{3,2,1,0:T(8,128)S(1)}, bf16[512,112]{1,0:T(8...) custom-call(bf16[10,32,8,128]{3,2,1,0:T(8,128)(2,1)S(1)} %get-tuple-element.47., ...), custom_call_target="tpu_custom_call" | custom-call | flops 536870912 | bytes 16777216 | tf_op jit(solution)/shard_map/forward/pallas_call | solution.py:463
  20.9 1.7 %collective-permute-done.3.cols_hi = f32[8,128]{1,0:T(8,128)S(1)} collective-permute-done((f32[8,128]{1,0:T(8,128)}, f32[8,128]{1,0:T(8,128)S(1)}, u32[]{:S(2)}, u32[]{:S(2)}) %collective-permute-start.3) | collective-permute-done | bytes 4128 | tf_op jit(solution)/shard_map/ppermute | solution.py:388
  22.6 0.0 collective-permute-done.rows_lo
  22.6 0.0 collective-permute-done.1.rows_hi
  22.6 18.5 %steps.1 = (f32[2,32,8,128]{3,2,1,0:T(8,128)S(1)}, f32[2,32,8,128]{3,2,1,0:T(8,128)S(1)}, f32[2,32,128]{2,1,0:T(8,128)S(1)}, f32[2,32,128]{2,1,0:T(8,128)S(1)}, ...) custom-call(bf16[10,32,8,128]{3,2,1,0:T(8,128)(2,1)S(1)} %get-tuple-element.47.desc, ...), custom_call_target="tpu_custom_call" | custom-call | flops 2147483648 | bytes 16777216 | tf_op jit(solution)/shard_map/steps/pallas_call | solution.py:473
  41.1 10.5 %all_to_all.15 = f32[8,48,128]{2,1,0:T(8,128)S(1)} all-to-all(f32[8,48,128]{2,1,0:T(8,128)S(1)} %get-tuple-element.77), channel_id=1, replica_groups={{0,1,8,9,16,17,24,25},{64,65,72,73,80,81,88,89},{128,129,136,137,144,14..., dimensions={0} | all-to-all | bytes 393216 | tf_op jit(solution)/shard_map/all_to_all | solution.py:420
  51.7 11.8 %all_to_all.16 = f32[8,48,128]{2,1,0:T(8,128)S(1)} all-to-all(f32[8,48,128]{2,1,0:T(8,128)S(1)} %broadcast_in_dim.20), channel_id=1, replica_groups={{0,32,2,34,4,36,6,38},{1,33,3,35,5,37,7,39},{64,96,66,98,68,100,70,102}..., dimensions={0} | all-to-all | bytes 393216 | tf_op jit(solution)/shard_map/all_to_all | solution.py:420
  63.5 0.7 broadcast_in_dim.21
  64.2 11.7 %all-to-all-start.2 = ((f32[8,48,128]{2,1,0:T(8,128)}), f32[8,48,128]{2,1,0:T(8,128)S(1)}, u32[]{:S(2)}, u32[]{:S(2)}) async-start(f32[8,48,128]{2,1,0:T(8,128)} %broadcast_in_dim.21), calls=%async_computation.2 | async-start | bytes 393216 | tf_op jit(solution)/shard_map/all_to_all | solution.py:420
  76.0 5.5 %collective-permute-start.4 = (f32[2,32,128]{2,1,0:T(8,128)S(1)}, f32[2,32,128]{2,1,0:T(8,128)S(1)}, u32[]{:S(2)}, u32[]{:S(2)}) collective-permute-start(f32[2,32,128]{2,1,0:T(8,128)S(1)} %get-tuple-element.73), channel_id=1, source_target_pairs={{0,32},{32,64},{64,96},{96,128},{128,160},{160,192},{192,224},{224... | collective-permute-start | bytes 98312 | tf_op jit(solution)/shard_map/ppermute | solution.py:388
  81.5 1.9 %collective-permute-start.5 = (f32[2,32,128]{2,1,0:T(8,128)S(1)}, f32[2,32,128]{2,1,0:T(8,128)S(1)}, u32[]{:S(2)}, u32[]{:S(2)}) collective-permute-start(f32[2,32,128]{2,1,0:T(8,128)S(1)} %get-tuple-element.74), channel_id=1, source_target_pairs={{32,0},{64,32},{96,64},{128,96},{160,128},{192,160},{224,192},{256... | collective-permute-start | bytes 98312 | tf_op jit(solution)/shard_map/ppermute | solution.py:388
  83.4 7.5 %collective-permute-start.6 = (f32[8,128]{1,0:T(8,128)S(1)}, f32[8,128]{1,0:T(8,128)S(1)}, u32[]{:S(2)}, u32[]{:S(2)}) collective-permute-start(f32[8,128]{1,0:T(8,128)S(1)} %get-tuple-element.75), channel_id=1, source_target_pairs={{0,1},{1,2},{2,3},{3,4},{4,5},{5,6},{6,7},{7,8},{8,9},{9,10},{10,1... | collective-permute-start | bytes 12296 | tf_op jit(solution)/shard_map/ppermute | solution.py:388
  90.9 1.9 %collective-permute-start.7 = (f32[8,128]{1,0:T(8,128)S(1)}, f32[8,128]{1,0:T(8,128)S(1)}, u32[]{:S(2)}, u32[]{:S(2)}) collective-permute-start(f32[8,128]{1,0:T(8,128)S(1)} %get-tuple-element.76), channel_id=1, source_target_pairs={{1,0},{2,1},{3,2},{4,3},{5,4},{6,5},{7,6},{8,7},{9,8},{10,9},{11,1... | collective-permute-start | bytes 12296 | tf_op jit(solution)/shard_map/ppermute | solution.py:388
  92.9 6.0 %collective-permute-done.7.cols_hi = f32[8,128]{1,0:T(8,128)S(1)} collective-permute-done((f32[8,128]{1,0:T(8,128)S(1)}, f32[8,128]{1,0:T(8,128)S(1)}, u32[]{:S(2)}, u32[]{:S(2)}) %collective-permute-start.7) | collective-permute-done | bytes 4128 | tf_op jit(solution)/shard_map/ppermute | solution.py:388
  98.9 1.6 %finish.1 = (f32[32,8,128]{2,1,0:T(8,128)}, f32[32,8,128]{2,1,0:T(8,128)}, f32[12,64]{1,0:T(8,128)}, f32[1,64]{1,0:T(1,128)}, f32[64,64]{1,0:T(8,128)}, /*index=...) custom-call(f32[2,32,8,128]{3,2,1,0:T(8,128)S(1)} %get-tuple-element.71.part, f32[2,32,8,128]{3,2,1,0:T(8,128)S(1)} %get-tuple-element.72.push, ...), custom_call_target="tpu_custom_call" | custom-call | tf_op jit(solution)/shard_map/finish/pallas_call | solution.py:506
  (11 shorter events, 0.1 us)
Async XLA Ops:
  4.4 18.2 %copy-start = (f32[4]{0:T(128)S(1)}, f32[4]{0:T(128)}, u32[]{:S(2)}) copy-start(f32[4]{0:T(128)} %cond_s.3) | copy-start | bytes 52
  4.4 18.2 %copy-start.1 = (f32[4]{0:T(128)S(1)}, f32[4]{0:T(128)}, u32[]{:S(2)}) copy-start(f32[4]{0:T(128)} %cond_f.3) | copy-start | bytes 52
  4.4 18.2 %collective-permute-start = (f32[4,32,128]{2,1,0:T(8,128)}, f32[4,32,128]{2,1,0:T(8,128)S(1)}, u32[]{:S(2)}, u32[]{:S(2)}) collective-permute-start(f32[4,32,128]{2,1,0:T(8,128)} %get-tuple-element.55), channel_id=1, source_target_pairs={{0,32},{32,64},{64,96},{96,128},{128,160},{160,192},{192,224},{224... | collective-permute-start | bytes 196616 | tf_op jit(solution)/shard_map/ppermute | solution.py:388
  9.2 13.4 %collective-permute-start.1 = (f32[4,32,128]{2,1,0:T(8,128)}, f32[4,32,128]{2,1,0:T(8,128)S(1)}, u32[]{:S(2)}, u32[]{:S(2)}) collective-permute-start(f32[4,32,128]{2,1,0:T(8,128)} %get-tuple-element.56), channel_id=1, source_target_pairs={{32,0},{64,32},{96,64},{128,96},{160,128},{192,160},{224,192},{256... | collective-permute-start | bytes 196616 | tf_op jit(solution)/shard_map/ppermute | solution.py:388
  11.1 9.8 %collective-permute-start.2 = (f32[8,128]{1,0:T(8,128)}, f32[8,128]{1,0:T(8,128)S(1)}, u32[]{:S(2)}, u32[]{:S(2)}) collective-permute-start(f32[8,128]{1,0:T(8,128)} %get-tuple-element.57), channel_id=1, source_target_pairs={{0,1},{1,2},{2,3},{3,4},{4,5},{5,6},{6,7},{7,8},{8,9},{9,10},{10,1... | collective-permute-start | bytes 12296 | tf_op jit(solution)/shard_map/ppermute | solution.py:388
  14.4 8.1 %collective-permute-start.3 = (f32[8,128]{1,0:T(8,128)}, f32[8,128]{1,0:T(8,128)S(1)}, u32[]{:S(2)}, u32[]{:S(2)}) collective-permute-start(f32[8,128]{1,0:T(8,128)} %get-tuple-element.58), channel_id=1, source_target_pairs={{1,0},{2,1},{3,2},{4,3},{5,4},{6,5},{7,6},{8,7},{9,8},{10,9},{11,1... | collective-permute-start | bytes 12296 | tf_op jit(solution)/shard_map/ppermute | solution.py:388
  16.3 0.7 copy-start.2
  64.2 28.7 %all-to-all-start.2 = ((f32[8,48,128]{2,1,0:T(8,128)}), f32[8,48,128]{2,1,0:T(8,128)S(1)}, u32[]{:S(2)}, u32[]{:S(2)}) async-start(f32[8,48,128]{2,1,0:T(8,128)} %broadcast_in_dim.21), calls=%async_computation.2 | async-start | bytes 393216 | tf_op jit(solution)/shard_map/all_to_all | solution.py:420
  76.0 22.9 %collective-permute-start.4 = (f32[2,32,128]{2,1,0:T(8,128)S(1)}, f32[2,32,128]{2,1,0:T(8,128)S(1)}, u32[]{:S(2)}, u32[]{:S(2)}) collective-permute-start(f32[2,32,128]{2,1,0:T(8,128)S(1)} %get-tuple-element.73), channel_id=1, source_target_pairs={{0,32},{32,64},{64,96},{96,128},{128,160},{160,192},{192,224},{224... | collective-permute-start | bytes 98312 | tf_op jit(solution)/shard_map/ppermute | solution.py:388
  81.5 17.4 %collective-permute-start.5 = (f32[2,32,128]{2,1,0:T(8,128)S(1)}, f32[2,32,128]{2,1,0:T(8,128)S(1)}, u32[]{:S(2)}, u32[]{:S(2)}) collective-permute-start(f32[2,32,128]{2,1,0:T(8,128)S(1)} %get-tuple-element.74), channel_id=1, source_target_pairs={{32,0},{64,32},{96,64},{128,96},{160,128},{192,160},{224,192},{256... | collective-permute-start | bytes 98312 | tf_op jit(solution)/shard_map/ppermute | solution.py:388
  83.4 9.5 %collective-permute-start.6 = (f32[8,128]{1,0:T(8,128)S(1)}, f32[8,128]{1,0:T(8,128)S(1)}, u32[]{:S(2)}, u32[]{:S(2)}) collective-permute-start(f32[8,128]{1,0:T(8,128)S(1)} %get-tuple-element.75), channel_id=1, source_target_pairs={{0,1},{1,2},{2,3},{3,4},{4,5},{5,6},{6,7},{7,8},{8,9},{9,10},{10,1... | collective-permute-start | bytes 12296 | tf_op jit(solution)/shard_map/ppermute | solution.py:388
  90.9 7.9 %collective-permute-start.7 = (f32[8,128]{1,0:T(8,128)S(1)}, f32[8,128]{1,0:T(8,128)S(1)}, u32[]{:S(2)}, u32[]{:S(2)}) collective-permute-start(f32[8,128]{1,0:T(8,128)S(1)} %get-tuple-element.76), channel_id=1, source_target_pairs={{1,0},{2,1},{3,2},{4,3},{5,4},{6,5},{7,6},{8,7},{9,8},{10,9},{11,1... | collective-permute-start | bytes 12296 | tf_op jit(solution)/shard_map/ppermute | solution.py:388

commit v3 on v2

--- a/solution.py
+++ b/solution.py
@@ -10,7 +10,7 @@
 
 time_step = 0.15
 loss_gain = 16.0
-LOADED = 12
+LOADED = 13
 DESC, HID, XB, YB = 10, 64, 8, 128
 ONES = DESC * XB + 2 * XB
 KF = ONES + 16
@@ -56,11 +56,13 @@
             v = field(z)
             spot = f * depth + z
             lo = jnp.where(lane == spot, pltpu.roll(v, spot, 1), lo)
-            hi = jnp.where(lane == spot, pltpu.roll(v, lax.rem(spot + 1, YB), 1), hi)
+            hi = jnp.where(lane == spot, pltpu.roll(v, (spot + 1) % YB, 1), hi)
         return lo, hi
 
     zero = jnp.zeros((XB, YB), F32)
-    lo, hi = lax.fori_loop(0, depth, one, (zero, zero), unroll=4)
+    lo, hi = zero, zero
+    for z in range(depth):
+        lo, hi = one(z, (lo, hi))
     lo_ref[...] = lo
     hi_ref[...] = hi
 
@@ -156,7 +158,7 @@
     h1, h2 = jnp.concatenate(h1, axis=0), jnp.concatenate(h2, axis=0)
     logits = nn(out[...], h2)
     yield
-    return h1, h2, logits[:XB] + bias_out[0], logits[XB:] + bias_out[1]
+    return h1, h2, logits[:XB] + bias_out[:, :1], logits[XB:] + bias_out[:, 1:]
 
 
 def softplus_terms(v):
@@ -209,7 +211,7 @@
     spot = f * depth + z
     above = jnp.broadcast_to(rows_lo[f, pl.ds(z, 1), :], (XB, YB))
     below = jnp.broadcast_to(rows_hi[f, pl.ds(z, 1), :], (XB, YB))
-    left = pltpu.roll(cols_lo[...], lax.rem(YB - spot, YB), 1)
+    left = pltpu.roll(cols_lo[...], (YB - spot) % YB, 1)
     right = pltpu.roll(cols_hi[...], YB - 1 - spot, 1)
     return above, below, left, right
 
@@ -369,7 +371,8 @@
             adj[z] = part[f, z] + laplace(push[f, z], *rim(f, z, depth, *rims))
         return 0
 
-    lax.fori_loop(0, depth, one, 0, unroll=4)
+    for z in range(depth):
+        one(z, 0)
     half = HID // 2
     g_w_mid[:half, :] = summed[:half, :HID] * scale
     g_w_mid[half:, :] = summed[:half, HID:] * scale
@@ -434,7 +437,7 @@
     rows, column = (4, depth, YB), (XB, YB)
     given = (
         solid_temp, fluid_temp, material, fixed_mask, solid_cot, fluid_cot,
-        descriptors, w_in, b_in[None], w_mid, b_mid[None], w_out.T,
+        descriptors, w_in, b_in[None], w_mid, b_mid[None], w_out.T, b_out[None],
     )
     *loaded, row_lo, row_hi, col_lo, col_hi, push = pl.pallas_call(
         edges_kernel,
@@ -463,12 +466,12 @@
     saved = pl.pallas_call(
         forward_kernel,
         out_shape=kept,
-        in_specs=[VMEM] * 8 + [SMEM],
+        in_specs=[VMEM] * 9,
         out_specs=[VMEM] * len(kept),
         cost_estimate=pl.CostEstimate(flops=2**29, bytes_accessed=2**24, transcendentals=2**22),
         name="forward",
         compiler_params=pltpu.CompilerParams(vmem_limit_bytes=24 * 2**20),
-    )(desc, solid, fluid, *weights, b_out)
+    )(desc, solid, fluid, *weights)
 
     part, later_push, *edges, payload = pl.pallas_call(
         steps_kernel,
@@ -481,7 +484,7 @@
             shape(column),
             shape((len(rings()[0][0]), 48, YB)),
         ],
-        in_specs=[VMEM] * 5 + [SMEM] * 2 + [VMEM] * 15 + [SMEM],
+        in_specs=[VMEM] * 5 + [SMEM] * 2 + [VMEM] * 16,
         out_specs=[VMEM] * 7,
         scratch_shapes=[
             pltpu.VMEM((WIDE, 2 * XB), BF),
@@ -496,7 +499,7 @@
         compiler_params=pltpu.CompilerParams(vmem_limit_bytes=32 * 2**20),
     )(
         desc, solid, fluid, material, fixed, solid_cond, fluid_cond,
-        cot_s, cot_f, push, *received, *saved, weights[0], b_out,
+        cot_s, cot_f, push, *received, *saved, weights[0], weights[-1],
     )
     received = exchange(*edges)
     summed = total_over_devices(payload)

time: 101 us -> 97.9 us (0.969)
  Pallas kernels: 27.8 us -> 25.3 us
  blocking collectives: 22.4 us -> 21.2 us
  waiting for transfers between devices: 7.64 us -> 8.83 us
    ppermute x8, waiting for transfers between devices: 7.64 us -> 8.83 us  [shift(): return lax.ppermute(value, axis, pairs)]
    all_to_all x2, blocking collectives: 22.4 us -> 21.2 us  [total_over_devices(): lax.all_to_all(copies, axes, 0, 0, axis_index_groups=members).sum(0)]
  transfers between devices with their start and end apart: 9 -> 9, of which waited for: 2 -> 2; matrix products, arithmetic and copies ran while one was open for 0% -> 0% of each run, Pallas kernels for 4% -> 3%
where the time goes in v3:
time: 97.9 us; the launch traced here: 97.4 us
  starting transfers between devices  40.5 us (41%)
  Pallas kernels  25.3 us (26%)
  blocking collectives  21.2 us (22%)
  waiting for transfers between devices  8.83 us (9%)
    ppermute x8, starting transfers between devices, shift(): return lax.ppermute(value, axis, pairs)  28.8 us
    all_to_all x2, blocking collectives, total_over_devices(): lax.all_to_all(copies, axes, 0, 0, axis_index_groups=members).sum(0)  21.2 us
    pallas_call x1, Pallas kernels, shards(): pl.pallas_call(steps_kernel, out_shape=[shape((2,) + field), shape((2,) +...  17.8 us
    all_to_all x1, starting transfers between devices, total_over_devices(): lax.all_to_all(copies, axes, 0, 0, axis_index_groups=members).sum(0)  11.7 us
    ppermute x8, waiting for transfers between devices, shift(): return lax.ppermute(value, axis, pairs)  8.83 us
    pallas_call x1, Pallas kernels, shards(): pl.pallas_call(forward_kernel, out_shape=kept, in_specs=[VMEM] * 9, out_s...  3.36 us
    pallas_call x1, Pallas kernels, shards(): pl.pallas_call(edges_kernel, out_shape=[pltpu.VMEM(v.shape, v.dtype) for...  3.08 us
  transfers between devices with their start and end apart: 9, of which 2 were waited for; matrix products, arithmetic and copies ran while one was open for 0% of the time, Pallas kernels for 3%

profile of v3, /device:TPU:57, one launch (start us, length us, event | category | flops | bytes accessed | tf_op | source)
XLA Modules:
  0.0 97.4 jit_solution(13067721746244619918)
XLA Ops:
  0.6 3.1 %edges.1 = (f32[32,8,128]{2,1,0:T(8,128)S(1)}, f32[32,8,128]{2,1,0:T(8,128)S(1)}, s32[32,8,128]{2,1,0:T(8,128)S(1)}, s32[32,8,128]{2,1,0:T(8,128)S(1)}, f32[32,8...) custom-call(f32[4]{0:T(128)} %cond_s.3, f32[4]{0:T(128)} %cond_f.3, ...), custom_call_target="tpu_custom_call" | custom-call | tf_op jit(solution)/shard_map/edges/pallas_call | solution.py:442
  3.7 0.0 copy-start
  3.7 0.0 copy-start.1
  3.7 4.8 %collective-permute-start = (f32[4,32,128]{2,1,0:T(8,128)}, f32[4,32,128]{2,1,0:T(8,128)S(1)}, u32[]{:S(2)}, u32[]{:S(2)}) collective-permute-start(f32[4,32,128]{2,1,0:T(8,128)} %get-tuple-element.56), channel_id=1, source_target_pairs={{0,32},{32,64},{64,96},{96,128},{128,160},{160,192},{192,224},{224... | collective-permute-start | bytes 196616 | tf_op jit(solution)/shard_map/ppermute | solution.py:391
  8.5 1.9 %collective-permute-start.1 = (f32[4,32,128]{2,1,0:T(8,128)}, f32[4,32,128]{2,1,0:T(8,128)S(1)}, u32[]{:S(2)}, u32[]{:S(2)}) collective-permute-start(f32[4,32,128]{2,1,0:T(8,128)} %get-tuple-element.57), channel_id=1, source_target_pairs={{32,0},{64,32},{96,64},{128,96},{160,128},{192,160},{224,192},{256... | collective-permute-start | bytes 196616 | tf_op jit(solution)/shard_map/ppermute | solution.py:391
  10.5 3.3 %collective-permute-start.2 = (f32[8,128]{1,0:T(8,128)}, f32[8,128]{1,0:T(8,128)S(1)}, u32[]{:S(2)}, u32[]{:S(2)}) collective-permute-start(f32[8,128]{1,0:T(8,128)} %get-tuple-element.58), channel_id=1, source_target_pairs={{0,1},{1,2},{2,3},{3,4},{4,5},{5,6},{6,7},{7,8},{8,9},{9,10},{10,1... | collective-permute-start | bytes 12296 | tf_op jit(solution)/shard_map/ppermute | solution.py:391
  13.8 1.9 %collective-permute-start.3 = (f32[8,128]{1,0:T(8,128)}, f32[8,128]{1,0:T(8,128)S(1)}, u32[]{:S(2)}, u32[]{:S(2)}) collective-permute-start(f32[8,128]{1,0:T(8,128)} %get-tuple-element.59), channel_id=1, source_target_pairs={{1,0},{2,1},{3,2},{4,3},{5,4},{6,5},{7,6},{8,7},{9,8},{10,9},{11,1... | collective-permute-start | bytes 12296 | tf_op jit(solution)/shard_map/ppermute | solution.py:391
  15.7 3.4 %forward.1 = (bf16[16,512,256]{2,1,0:T(8,128)(2,1)S(1)}, bf16[16,512,256]{2,1,0:T(8,128)(2,1)S(1)}, f32[16,2,8,256]{3,2,1,0:T(8,128)S(1)}, bf16[512,112]{1,0:T(8...) custom-call(bf16[10,32,8,128]{3,2,1,0:T(8,128)(2,1)S(1)} %get-tuple-element.48., ...), custom_call_target="tpu_custom_call" | custom-call | flops 536870912 | bytes 16777216 | tf_op jit(solution)/shard_map/forward/pallas_call | solution.py:466
  19.0 2.9 %collective-permute-done.3.cols_hi = f32[8,128]{1,0:T(8,128)S(1)} collective-permute-done((f32[8,128]{1,0:T(8,128)}, f32[8,128]{1,0:T(8,128)S(1)}, u32[]{:S(2)}, u32[]{:S(2)}) %collective-permute-start.3) | collective-permute-done | bytes 4128 | tf_op jit(solution)/shard_map/ppermute | solution.py:391
  21.9 0.0 collective-permute-done.rows_lo
  21.9 0.0 collective-permute-done.1.rows_hi
  21.9 17.8 %steps.1 = (f32[2,32,8,128]{3,2,1,0:T(8,128)S(1)}, f32[2,32,8,128]{3,2,1,0:T(8,128)S(1)}, f32[2,32,128]{2,1,0:T(8,128)S(1)}, f32[2,32,128]{2,1,0:T(8,128)S(1)}, ...) custom-call(bf16[10,32,8,128]{3,2,1,0:T(8,128)(2,1)S(1)} %get-tuple-element.48.desc, ...), custom_call_target="tpu_custom_call" | custom-call | flops 2147483648 | bytes 16777216 | tf_op jit(solution)/shard_map/steps/pallas_call | solution.py:476
  39.7 9.8 %all_to_all.15 = f32[8,48,128]{2,1,0:T(8,128)S(1)} all-to-all(f32[8,48,128]{2,1,0:T(8,128)S(1)} %get-tuple-element.79), channel_id=1, replica_groups={{0,1,8,9,16,17,24,25},{64,65,72,73,80,81,88,89},{128,129,136,137,144,14..., dimensions={0} | all-to-all | bytes 393216 | tf_op jit(solution)/shard_map/all_to_all | solution.py:423
  49.5 11.4 %all_to_all.16 = f32[8,48,128]{2,1,0:T(8,128)S(1)} all-to-all(f32[8,48,128]{2,1,0:T(8,128)S(1)} %broadcast_in_dim.24), channel_id=1, replica_groups={{0,32,2,34,4,36,6,38},{1,33,3,35,5,37,7,39},{64,96,66,98,68,100,70,102}..., dimensions={0} | all-to-all | bytes 393216 | tf_op jit(solution)/shard_map/all_to_all | solution.py:423
  60.9 0.7 broadcast_in_dim.25
  61.6 11.7 %all-to-all-start.2 = ((f32[8,48,128]{2,1,0:T(8,128)}), f32[8,48,128]{2,1,0:T(8,128)S(1)}, u32[]{:S(2)}, u32[]{:S(2)}) async-start(f32[8,48,128]{2,1,0:T(8,128)} %broadcast_in_dim.25), calls=%async_computation.2 | async-start | bytes 393216 | tf_op jit(solution)/shard_map/all_to_all | solution.py:423
  73.4 5.5 %collective-permute-start.4 = (f32[2,32,128]{2,1,0:T(8,128)S(1)}, f32[2,32,128]{2,1,0:T(8,128)S(1)}, u32[]{:S(2)}, u32[]{:S(2)}) collective-permute-start(f32[2,32,128]{2,1,0:T(8,128)S(1)} %get-tuple-element.75), channel_id=1, source_target_pairs={{0,32},{32,64},{64,96},{96,128},{128,160},{160,192},{192,224},{224... | collective-permute-start | bytes 98312 | tf_op jit(solution)/shard_map/ppermute | solution.py:391
  78.9 1.9 %collective-permute-start.5 = (f32[2,32,128]{2,1,0:T(8,128)S(1)}, f32[2,32,128]{2,1,0:T(8,128)S(1)}, u32[]{:S(2)}, u32[]{:S(2)}) collective-permute-start(f32[2,32,128]{2,1,0:T(8,128)S(1)} %get-tuple-element.76), channel_id=1, source_target_pairs={{32,0},{64,32},{96,64},{128,96},{160,128},{192,160},{224,192},{256... | collective-permute-start | bytes 98312 | tf_op jit(solution)/shard_map/ppermute | solution.py:391
  80.8 7.5 %collective-permute-start.6 = (f32[8,128]{1,0:T(8,128)S(1)}, f32[8,128]{1,0:T(8,128)S(1)}, u32[]{:S(2)}, u32[]{:S(2)}) collective-permute-start(f32[8,128]{1,0:T(8,128)S(1)} %get-tuple-element.77), channel_id=1, source_target_pairs={{0,1},{1,2},{2,3},{3,4},{4,5},{5,6},{6,7},{7,8},{8,9},{9,10},{10,1... | collective-permute-start | bytes 12296 | tf_op jit(solution)/shard_map/ppermute | solution.py:391
  88.3 1.9 %collective-permute-start.7 = (f32[8,128]{1,0:T(8,128)S(1)}, f32[8,128]{1,0:T(8,128)S(1)}, u32[]{:S(2)}, u32[]{:S(2)}) collective-permute-start(f32[8,128]{1,0:T(8,128)S(1)} %get-tuple-element.78), channel_id=1, source_target_pairs={{1,0},{2,1},{3,2},{4,3},{5,4},{6,5},{7,6},{8,7},{9,8},{10,9},{11,1... | collective-permute-start | bytes 12296 | tf_op jit(solution)/shard_map/ppermute | solution.py:391
  90.3 0.0 all-to-all-done.2
  90.3 0.0 collective-permute-done.6.cols_lo
  90.3 6.0 %collective-permute-done.7.cols_hi = f32[8,128]{1,0:T(8,128)S(1)} collective-permute-done((f32[8,128]{1,0:T(8,128)S(1)}, f32[8,128]{1,0:T(8,128)S(1)}, u32[]{:S(2)}, u32[]{:S(2)}) %collective-permute-start.7) | collective-permute-done | bytes 4128 | tf_op jit(solution)/shard_map/ppermute | solution.py:391
  96.3 1.1 %finish.1 = (f32[32,8,128]{2,1,0:T(8,128)}, f32[32,8,128]{2,1,0:T(8,128)}, f32[12,64]{1,0:T(8,128)}, f32[1,64]{1,0:T(1,128)}, f32[64,64]{1,0:T(8,128)}, /*index=...) custom-call(f32[2,32,8,128]{3,2,1,0:T(8,128)S(1)} %get-tuple-element.73.part, f32[2,32,8,128]{3,2,1,0:T(8,128)S(1)} %get-tuple-element.74.push, ...), custom_call_target="tpu_custom_call" | custom-call | tf_op jit(solution)/shard_map/finish/pallas_call | solution.py:509
  (9 shorter events, 0.1 us)
Async XLA Ops:
  3.7 18.2 %copy-start = (f32[4]{0:T(128)S(1)}, f32[4]{0:T(128)}, u32[]{:S(2)}) copy-start(f32[4]{0:T(128)} %cond_s.3) | copy-start | bytes 52
  3.7 18.2 %copy-start.1 = (f32[4]{0:T(128)S(1)}, f32[4]{0:T(128)}, u32[]{:S(2)}) copy-start(f32[4]{0:T(128)} %cond_f.3) | copy-start | bytes 52
  3.7 18.2 %collective-permute-start = (f32[4,32,128]{2,1,0:T(8,128)}, f32[4,32,128]{2,1,0:T(8,128)S(1)}, u32[]{:S(2)}, u32[]{:S(2)}) collective-permute-start(f32[4,32,128]{2,1,0:T(8,128)} %get-tuple-element.56), channel_id=1, source_target_pairs={{0,32},{32,64},{64,96},{96,128},{128,160},{160,192},{192,224},{224... | collective-permute-start | bytes 196616 | tf_op jit(solution)/shard_map/ppermute | solution.py:391
  8.5 13.4 %collective-permute-start.1 = (f32[4,32,128]{2,1,0:T(8,128)}, f32[4,32,128]{2,1,0:T(8,128)S(1)}, u32[]{:S(2)}, u32[]{:S(2)}) collective-permute-start(f32[4,32,128]{2,1,0:T(8,128)} %get-tuple-element.57), channel_id=1, source_target_pairs={{32,0},{64,32},{96,64},{128,96},{160,128},{192,160},{224,192},{256... | collective-permute-start | bytes 196616 | tf_op jit(solution)/shard_map/ppermute | solution.py:391
  10.5 8.6 %collective-permute-start.2 = (f32[8,128]{1,0:T(8,128)}, f32[8,128]{1,0:T(8,128)S(1)}, u32[]{:S(2)}, u32[]{:S(2)}) collective-permute-start(f32[8,128]{1,0:T(8,128)} %get-tuple-element.58), channel_id=1, source_target_pairs={{0,1},{1,2},{2,3},{3,4},{4,5},{5,6},{6,7},{7,8},{8,9},{9,10},{10,1... | collective-permute-start | bytes 12296 | tf_op jit(solution)/shard_map/ppermute | solution.py:391
  13.8 8.1 %collective-permute-start.3 = (f32[8,128]{1,0:T(8,128)}, f32[8,128]{1,0:T(8,128)S(1)}, u32[]{:S(2)}, u32[]{:S(2)}) collective-permute-start(f32[8,128]{1,0:T(8,128)} %get-tuple-element.59), channel_id=1, source_target_pairs={{1,0},{2,1},{3,2},{4,3},{5,4},{6,5},{7,6},{8,7},{9,8},{10,9},{11,1... | collective-permute-start | bytes 12296 | tf_op jit(solution)/shard_map/ppermute | solution.py:391
  61.6 28.6 %all-to-all-start.2 = ((f32[8,48,128]{2,1,0:T(8,128)}), f32[8,48,128]{2,1,0:T(8,128)S(1)}, u32[]{:S(2)}, u32[]{:S(2)}) async-start(f32[8,48,128]{2,1,0:T(8,128)} %broadcast_in_dim.25), calls=%async_computation.2 | async-start | bytes 393216 | tf_op jit(solution)/shard_map/all_to_all | solution.py:423
  73.4 22.9 %collective-permute-start.4 = (f32[2,32,128]{2,1,0:T(8,128)S(1)}, f32[2,32,128]{2,1,0:T(8,128)S(1)}, u32[]{:S(2)}, u32[]{:S(2)}) collective-permute-start(f32[2,32,128]{2,1,0:T(8,128)S(1)} %get-tuple-element.75), channel_id=1, source_target_pairs={{0,32},{32,64},{64,96},{96,128},{128,160},{160,192},{192,224},{224... | collective-permute-start | bytes 98312 | tf_op jit(solution)/shard_map/ppermute | solution.py:391
  78.9 17.4 %collective-permute-start.5 = (f32[2,32,128]{2,1,0:T(8,128)S(1)}, f32[2,32,128]{2,1,0:T(8,128)S(1)}, u32[]{:S(2)}, u32[]{:S(2)}) collective-permute-start(f32[2,32,128]{2,1,0:T(8,128)S(1)} %get-tuple-element.76), channel_id=1, source_target_pairs={{32,0},{64,32},{96,64},{128,96},{160,128},{192,160},{224,192},{256... | collective-permute-start | bytes 98312 | tf_op jit(solution)/shard_map/ppermute | solution.py:391
  80.8 9.5 %collective-permute-start.6 = (f32[8,128]{1,0:T(8,128)S(1)}, f32[8,128]{1,0:T(8,128)S(1)}, u32[]{:S(2)}, u32[]{:S(2)}) collective-permute-start(f32[8,128]{1,0:T(8,128)S(1)} %get-tuple-element.77), channel_id=1, source_target_pairs={{0,1},{1,2},{2,3},{3,4},{4,5},{5,6},{6,7},{7,8},{8,9},{9,10},{10,1... | collective-permute-start | bytes 12296 | tf_op jit(solution)/shard_map/ppermute | solution.py:391
  88.3 7.9 %collective-permute-start.7 = (f32[8,128]{1,0:T(8,128)S(1)}, f32[8,128]{1,0:T(8,128)S(1)}, u32[]{:S(2)}, u32[]{:S(2)}) collective-permute-start(f32[8,128]{1,0:T(8,128)S(1)} %get-tuple-element.78), channel_id=1, source_target_pairs={{1,0},{2,1},{3,2},{4,3},{5,4},{6,5},{7,6},{8,7},{9,8},{10,9},{11,1... | collective-permute-start | bytes 12296 | tf_op jit(solution)/shard_map/ppermute | solution.py:391
